TPU v7x, 256 devices: a whole 4x4x8 slice. The times are simulated.
256 devices in a mesh: mem: 16 (over y, x), reg: 16 (over z, core).
Axes of the slice: x: 4, y: 4, z: 8, core: 2. Of those that a mesh axis runs over, the one named last changes fastest.
Arguments:
- prior_states: bfloat16 [256, 227, 8192], P('mem', None, 'reg'), may hold values from -6 to 6
- sensor_space_runs: bfloat16 [256, 16, 8192], P('mem', 'reg'), may hold values from -6 to 6
- sensor_readings: float32 [16, 8192], P('reg'), may hold values from -8 to 8
- noise_precision: float32 [16, 8192], P('reg'), may hold values from 0.1 to 1
- reading_pointers: int32 [16, 16, 4, 512], P('reg', 'mem'), may hold values from 0 to 8703, as said below
- reading_tally: int32 [16, 16, 4], P('reg', 'mem'), may hold values from 128 to 512, as said below
Outputs:
- analysis: bfloat16 [256, 227, 8192], P('mem', None, 'reg')
Inputs may be any that keep to these rules, and one draw needn't show every extreme that they name: Row reading_pointers[r, m, g, :] holds 512 distinct positions of region r's extended observations, together one window of 512 consecutive positions, in an order drawn from the seed. A local analysis uses the first reading_tally[r, m, g] entries of its list.
All inputs are finite; a program needn't handle non-finite values.
Results may differ from a plain program's by a relative error of at most 0.009.
Values may be sent and summed in bfloat16 or wider, within the bound.
No kernel may reach another device: no remote copies, remote signals or barrier semaphores. Data moves between devices by JAX's collectives and lax.ppermute only.
A program may use at most 128 MiB of HBM per device.

v0:
```python
import math

import jax
import jax.numpy as jnp
from jax import lax
from jax.sharding import PartitionSpec as P

NS_ITERS = 6
HW = 256


inflation = 1.1
highest = lax.Precision.HIGHEST


def with_halo(cells, sides, width):
    for axis, dim in sides:
        count = lax.axis_size(axis)
        head = lax.slice_in_dim(cells, 0, width, axis=dim)
        tail = lax.slice_in_dim(cells, cells.shape[dim] - width, cells.shape[dim], axis=dim)
        cells = jnp.concatenate(
            [
                lax.ppermute(tail, axis, [(i, (i + 1) % count) for i in range(count)]),
                cells,
                lax.ppermute(head, axis, [((i + 1) % count, i) for i in range(count)]),
            ],
            axis=dim,
        )
    return cells


def nearby_correction(
    prior_patch, sensor_space_lines, sensor_readings, precision_nearby, pending_amount
):
    runs_sequence = prior_patch.shape[0]
    prior_states_narrow = prior_patch.astype(jnp.float32)
    middle_pillar = jnp.mean(prior_states_narrow, axis=0)
    deviation_matrix = (prior_states_narrow - middle_pillar[None]).astype(jnp.bfloat16)
    observed_f32 = sensor_space_lines.astype(jnp.float32)
    ens_mean = jnp.mean(observed_f32, axis=0)
    anomaly = lax.optimization_barrier((observed_f32 - ens_mean[None]).astype(jnp.bfloat16)).astype(
        jnp.float32
    )
    active = (jnp.arange(sensor_space_lines.shape[1], dtype=jnp.int32) < pending_amount).astype(
        jnp.float32
    )
    weight = precision_nearby * active
    identity = jnp.eye(runs_sequence, dtype=jnp.float32)
    gram_matrix = (
        jnp.dot(anomaly, (anomaly * weight[None, :]).T, precision=highest)
        + (runs_sequence - 1) / inflation * identity
    )
    innovation_sum = jnp.dot(anomaly, weight * (sensor_readings - ens_mean), precision=highest)
    frobenius = jnp.sqrt(jnp.sum(gram_matrix * gram_matrix))
    iterate = gram_matrix / frobenius
    inverse_root = identity
    for iteration in range(NS_ITERS):
        factor = 1.5 * identity - 0.5 * jnp.dot(inverse_root, iterate, precision=highest)
        iterate = jnp.dot(iterate, factor, precision=highest)
        inverse_root = jnp.dot(factor, inverse_root, precision=highest)
    inverse_root = inverse_root / jnp.sqrt(frobenius)
    mean_weight = jnp.dot(
        inverse_root, jnp.dot(inverse_root, innovation_sum, precision=highest), precision=highest
    )
    transform = (math.sqrt(runs_sequence - 1) * inverse_root + mean_weight[:, None]).astype(
        jnp.bfloat16
    )
    combined = jnp.einsum(
        "jvc,jk->kvc",
        deviation_matrix.astype(jnp.float32),
        transform.astype(jnp.float32),
        precision=highest,
    )
    return (middle_pillar[None] + combined).astype(jnp.bfloat16)


def per_device(
    prior_states,
    sensor_space_runs,
    sensor_readings,
    noise_precision,
    reading_pointers,
    reading_tally,
):
    pillar_sequence = lax.all_to_all(prior_states, "mem", split_axis=2, concat_axis=0, tiled=True)
    runs_sequence, fields_sequence, columns_here = pillar_sequence.shape
    patch_amount = reading_tally.shape[2]
    patch_width = columns_here // patch_amount
    extended = with_halo(sensor_space_runs, (("reg", 2),), HW)
    statistics = jnp.stack([sensor_readings, noise_precision])
    stats_extended = with_halo(statistics.astype(jnp.bfloat16), (("reg", 2),), HW).astype(
        statistics.dtype
    )
    own_lists = reading_pointers[0, 0]
    gathered = lax.all_gather(extended, "mem", axis=0, tiled=True)
    sensor_space_lines = jnp.take(gathered[:, 0], own_lists.reshape(-1), axis=1)
    sensor_space_lines = sensor_space_lines.reshape(runs_sequence, patch_amount, -1)
    chosen_moments = jnp.take(stats_extended[:, 0], own_lists, axis=1)
    prior_patches = pillar_sequence.reshape(
        runs_sequence, fields_sequence, patch_amount, patch_width
    )
    analysed = jax.vmap(nearby_correction, in_axes=(2, 1, 0, 0, 0), out_axes=2)(
        prior_patches, sensor_space_lines, chosen_moments[0], chosen_moments[1], reading_tally[0, 0]
    )
    analysed = analysed.reshape(runs_sequence, fields_sequence, columns_here)
    return lax.all_to_all(analysed, "mem", split_axis=0, concat_axis=2, tiled=True)


def solution(mesh):
    placed = (
        P("mem", None, "reg"),
        P("mem", "reg", None),
        P("reg", None),
        P("reg", None),
        P("reg", "mem", None, None),
        P("reg", "mem", None),
    )
    return jax.shard_map(
        per_device, mesh=mesh, in_specs=placed, out_specs=P("mem", None, "reg"), check_vma=False
    )
```

profile of v0, /device:TPU:96, one launch (start us, length us, event | category | flops | bytes accessed | tf_op | source)
XLA Modules:
  0.0 244.3 jit_solution(5536810041124589090)
XLA Ops:
  6.5 0.7 fusion.45
  7.3 0.5 collective-permute-start
  7.8 0.9 collective-permute-done.1
  8.6 1.7 collective-permute-done
  10.3 1.7 pad_maximum_fusion
  12.0 8.4 %copy.29 = bf16[16,227,512]{1,0,2:T(8,128)(2,1)} copy(bf16[16,227,512]{2,0,1:T(8,128)(2,1)} %param.6) | data formatting | bytes 7438336 | tf_op args[0]
  20.4 7.2 %all-to-all-start = ((bf16[16,227,512]{1,0,2:T(8,128)(2,1)}), bf16[16,227,512]{1,0,2:T(8,128)(2,1)}, u32[]{:S(2)}, u32[]{:S(2)}) async-start(bf16[16,227,512]{1,0,2:T(8,128)(2,1)} %copy.29), calls=%async_computation | async-start | bytes 8388608 | tf_op jit(solution)/shard_map/all_to_all | solution.py:85
  27.8 1.2 collective-permute-start.2
  29.2 0.5 collective-permute-done.3
  29.7 1.1 collective-permute-done.2
  30.9 2.8 %copy.33 = f32[2,8704]{0,1:T(8,128)} copy(f32[2,8704]{1,0:T(2,128)S(1)} %maximum_convert_fusion) | data formatting | bytes 139264 | tf_op jit(solution)/shard_map/convert_element_type | solution.py:91
  33.6 7.7 %gather_fusion.1 = f32[2048,2]{1,0:T(8,128)S(1)} fusion(f32[2,8704]{0,1:T(8,128)} %copy.33, s32[2048]{0:T(1024)S(1)} %broadcast_clamp_fusion), kind=kCustom, calls=%fused_computation.1 | custom fusion | bytes 40960 | tf_op jit(solution)/shard_map/jit(_take)/gather | solution.py:98
  41.4 0.3 copy.34
  41.7 57.3 %all-to-all-done = bf16[16,227,512]{1,0,2:T(8,128)(2,1)} async-done(((bf16[16,227,512]{1,0,2:T(8,128)(2,1)}), bf16[16,227,512]{1,0,2:T(8,128)(2,1)}, u32[]{:S(2)}, u32[]{:S(2)}) %all-to-all-start) | async-done | bytes 3719200 | tf_op jit(solution)/shard_map/all_to_all | solution.py:85
  99.0 3.6 %copy_convert_fusion = f32[16,227,512]{1,2,0:T(8,128)S(1)} fusion(bf16[16,227,512]{1,0,2:T(8,128)(2,1)} %all-to-all-done), kind=kLoop, calls=%fused_computation.7 | loop fusion | flops 1859584 | bytes 11157504 | tf_op jit(solution)/shard_map/vmap()/convert_element_type | solution.py:36
  102.6 4.1 %copy.35 = f32[16,16,227,32]{2,3,1,0:T(8,128)} copy(f32[16,16,227,32]{2,3,0,1:T(8,128)S(1)} %bitcast.130) | data formatting | bytes 14876672 | tf_op jit(solution)/shard_map/vmap()/transpose | solution.py:38
  106.7 3.7 %fusion.8 = f32[227,512]{0,1:T(8,128)S(1)} fusion(bf16[16,227,512]{1,0,2:T(8,128)(2,1)} %all-to-all-done), kind=kLoop, calls=%fused_computation.13 | loop fusion | flops 3602944 | bytes 4184064 | tf_op jit(solution)/shard_map/vmap()/reduce_sum | solution.py:37
  110.5 6.7 %subtract_convert_fusion = bf16[4,256,227,8]{2,3,0,1:T(8,128)(2,1)} fusion(f32[4,256,227,8]{2,3,0,1:T(8,128)} %bitcast.129, f32[4,227,8]{1,2,0:T(8,128)S(1)} %get-tuple-element.15), kind=kLoop, calls=%fused_computation.2 | loop fusion | flops 3719168 | bytes 11186560 | tf_op jit(solution)/shard_map/vmap()/convert_element_type | solution.py:38
  117.2 6.6 %copy.31 = bf16[256,1,8704]{0,2,1:T(8,128)(2,1)} copy(bf16[256,1,8704]{2,0,1:T(8,128)(2,1)} %all-gather.2.cloned.1.call-done) | data formatting | bytes 8912896 | tf_op jit(solution)/shard_map/all_gather | solution.py:95
  123.8 9.5 %gather_fusion = bf16[2048,256]{1,0:T(8,128)(2,1)S(1)} fusion(bf16[256,8704]{0,1:T(8,128)(2,1)} %bitcast.128, s32[2048]{0:T(1024)S(1)} %broadcast_clamp_fusion.1), kind=kCustom, calls=%fused_computation | custom fusion | bytes 2105344 | tf_op jit(solution)/shard_map/jit(_take)/gather | solution.py:96
  133.3 0.7 convert_reduce_fusion
  134.1 0.7 copy.32
  135.2 1.5 multiply_reduce_fusion
  136.6 0.8 fusion.18
  137.5 0.6 fusion.28
  138.1 1.2 fusion.31
  139.3 1.2 fusion.16
  140.5 1.1 fusion.48
  141.7 1.1 fusion.49
  142.8 1.2 fusion.15
  144.0 1.1 fusion.50
  145.2 1.1 fusion.51
  146.4 1.4 fusion.14
  147.8 1.1 fusion.52
  148.9 1.1 fusion.53
  150.1 1.2 fusion.13
  151.3 1.1 fusion.54
  152.4 1.1 fusion.55
  153.6 0.9 fusion.37
  154.5 1.2 fusion.12
  155.7 1.1 convolution_divide_fusion
  156.9 1.0 fusion.41
  157.9 1.0 fusion.39
  158.9 5.6 %fusion = bf16[256,227,4,8]{0,1,3,2:T(8,128)(2,1)} fusion(f32[227,4,8]{0,2,1:T(8,128)S(1)} %get-tuple-element.16, bf16[4,256,227,8]{2,3,0,1:T(8,128)(2,1)S(1)} %copy-done, f32[4,256,256]{2,1,0:T(8,128)S(1)} %convolution_divide_fusion, f32[4,256]{1,0:T(4,128)S(1)} %bitcast.144), kind=kOutput, calls=%fused_computation.4 | convolution fusion | flops 956612608 | bytes 8520064 | tf_op jit(solution)/shard_map/vmap(jvc,jk->kvc)/dot_general | solution.py:68
  164.5 7.8 %copy.37 = bf16[256,227,32]{1,2,0:T(8,128)(2,1)} copy(bf16[256,227,32]{0,1,2:T(8,128)(2,1)} %bitcast.134) | data formatting | bytes 7438336 | tf_op jit(solution)/shard_map/reshape | solution.py:105
  172.3 55.4 %all_to_all.27 = bf16[256,227,32]{1,2,0:T(8,128)(2,1)S(1)} all-to-all(bf16[256,227,32]{1,2,0:T(8,128)(2,1)} %copy.37), channel_id=1, replica_groups=mesh['mem'=16,'reg'=16] {'mem'}, dimensions={0} | all-to-all | bytes 7438336 | tf_op jit(solution)/shard_map/all_to_all | solution.py:106
  227.8 2.4 copy.38
  230.2 7.3 %copy.39 = bf16[16,227,512]{2,0,1:T(8,128)(2,1)} copy(bf16[16,227,512]{1,2,0:T(8,128)(2,1)} %bitcast.132) | data formatting | bytes 7438336 | tf_op jit(solution)/shard_map/all_to_all | solution.py:106
  (40 shorter events, 0.7 us)
Async XLA Ops:
  6.5 110.7 %all-gather.2.cloned.1.call-start = ((), (), s32[]{:S(2)}) async-start(), calls=%async_computation.2 | async-start | bytes 4734976 | tf_op jit(solution)/shard_map/all_gather | solution.py:95
  7.3 1.4 collective-permute-start.1
  7.3 3.1 %collective-permute-start = (bf16[16,1,256]{2,0,1:T(8,128)(2,1)S(1)}, bf16[16,1,256]{2,0,1:T(8,128)(2,1)S(1)}, u32[]{:S(2)}, u32[]{:S(2)}) collective-permute-start(bf16[16,1,256]{2,0,1:T(8,128)(2,1)S(1)} %get-tuple-element.7), channel_id=1, source_target_pairs={{0,1},{1,2},{2,3},{3,4},{4,5},{5,6},{6,7},{7,8},{8,9},{9,10},{10,1... | collective-permute-start | bytes 24584 | tf_op jit(solution)/shard_map/ppermute | solution.py:23
  20.4 7.2 %copy-start.2 = (f32[1,8192]{1,0:T(1,128)S(1)}, f32[1,8192]{1,0:T(1,128)}, u32[]{:S(2)}) copy-start(f32[1,8192]{1,0:T(1,128)} %param.8) | copy-start | bytes 98308
  20.4 7.2 %copy-start.3 = (f32[1,8192]{1,0:T(1,128)S(1)}, f32[1,8192]{1,0:T(1,128)}, u32[]{:S(2)}) copy-start(f32[1,8192]{1,0:T(1,128)} %param.9) | copy-start | bytes 98308
  20.4 8.6 %copy-start.1 = (s32[1,1,4,512]{3,2,1,0:T(4,128)S(1)}, s32[1,1,4,512]{3,2,1,0:T(4,128)}, u32[]{:S(2)}) copy-start(s32[1,1,4,512]{3,2,1,0:T(4,128)} %param.10) | copy-start | bytes 24580
  20.4 78.6 %all-to-all-start = ((bf16[16,227,512]{1,0,2:T(8,128)(2,1)}), bf16[16,227,512]{1,0,2:T(8,128)(2,1)}, u32[]{:S(2)}, u32[]{:S(2)}) async-start(bf16[16,227,512]{1,0,2:T(8,128)(2,1)} %copy.29), calls=%async_computation | async-start | bytes 8388608 | tf_op jit(solution)/shard_map/all_to_all | solution.py:85
  27.8 1.9 collective-permute-start.3
  27.8 3.0 %collective-permute-start.2 = (bf16[2,1,256]{2,0,1:T(2,128)(2,1)S(1)}, bf16[2,1,256]{2,0,1:T(2,128)(2,1)S(1)}, u32[]{:S(2)}, u32[]{:S(2)}) collective-permute-start(bf16[2,1,256]{2,0,1:T(2,128)(2,1)S(1)} %get-tuple-element.9), channel_id=1, source_target_pairs={{0,1},{1,2},{2,3},{3,4},{4,5},{5,6},{6,7},{7,8},{8,9},{9,10},{10,1... | collective-permute-start | bytes 3080 | tf_op jit(solution)/shard_map/ppermute | solution.py:23
  133.3 1.8 copy-start.4
  154.5 4.4 %copy-start = (bf16[4,256,227,8]{2,3,0,1:T(8,128)(2,1)S(1)}, bf16[4,256,227,8]{2,3,0,1:T(8,128)(2,1)}, u32[]{:S(2)}) copy-start(bf16[4,256,227,8]{2,3,0,1:T(8,128)(2,1)} %subtract_convert_fusion) | copy-start | bytes 11157508
Sparse Core Ops, SparseCore 0:
  12.2 104.1 all-gather.1
where the time goes:
time: 245 us; the launch traced here: 244 us
  waiting for transfers between devices  61.4 us (25%)
  local copies, waits for them, and re-layouts  58.5 us (24%)
  blocking collectives  55.4 us (23%)
  matrix products  29.2 us (12%)
  other arithmetic  17.1 us (7%)
  between operations  13.8 us (6%)
  starting transfers between devices  8.99 us (4%)
    all_to_all x1, waiting for transfers between devices, per_device(): lax.all_to_all(prior_states, 'mem', split_axis=2, concat_axis=0, tiled=True)  57.3 us
    all_to_all x1, blocking collectives, per_device(): lax.all_to_all(analysed, 'mem', split_axis=0, concat_axis=2, tiled=True)  55.4 us
    gather x2, local copies, waits for them, and re-layouts, per_device(): sensor_space_lines = jnp.take(gathered[:, 0], own_lists.reshape(-1), axis=1)  10.2 us
    all_to_all x2, local copies, waits for them, and re-layouts, per_device(): lax.all_to_all(analysed, 'mem', split_axis=0, concat_axis=2, tiled=True)  9.72 us
    unnamed x14, local copies, waits for them, and re-layouts  8.41 us
    gather x2, local copies, waits for them, and re-layouts, per_device(): chosen_moments = jnp.take(stats_extended[:, 0], own_lists, axis=1)  8.07 us
    reshape x1, local copies, waits for them, and re-layouts, per_device(): analysed = analysed.reshape(runs_sequence, fields_sequence, columns_here)  7.84 us
    all_to_all x1, starting transfers between devices, per_device(): lax.all_to_all(prior_states, 'mem', split_axis=2, concat_axis=0, tiled=True)  7.22 us
  transfers between devices with their start and end apart: 6, of which 5 were waited for; matrix products, arithmetic and copies ran while one was open for 15% of the time, Pallas kernels for 0%

commit v1 on v0

v1 whole, which is shorter than its diff:
```python
import functools
import math

import jax
import jax.numpy as jnp
from jax import lax
from jax.experimental import pallas as pl
from jax.experimental.pallas import tpu as pltpu
from jax.sharding import PartitionSpec as P

NS_ITERS = 6
HW = 256
LANES = 128
INFLATION = 1.1
CHUNKS = 3


def swap_blocks(tiles):
    lane = lax.broadcasted_iota(jnp.int32, tiles[0].shape, 1)
    low_half = lane < 64
    even = (lane & 32) == 0
    turned = [pltpu.roll(t, 64, 1) for t in tiles]
    first = [
        jnp.where(low_half, tiles[0], turned[2]),
        jnp.where(low_half, tiles[1], turned[3]),
        jnp.where(low_half, turned[0], tiles[2]),
        jnp.where(low_half, turned[1], tiles[3]),
    ]
    out = []
    for a, b in ((first[0], first[1]), (first[2], first[3])):
        out.append(jnp.where(even, a, pltpu.roll(b, 32, 1)))
        out.append(jnp.where(even, pltpu.roll(a, 96, 1), b))
    return out


def pack_kernel(x_ref, o_ref):
    quads = o_ref.shape[1]

    def step(t, _):
        for u in range(4):
            tiles = [
                x_ref[4 * t + i, :, u * LANES : (u + 1) * LANES].astype(jnp.float32)
                for i in range(4)
            ]
            for d, tile in enumerate(swap_blocks(tiles)):
                o_ref[4 * u + d, t] = tile.astype(jnp.bfloat16)
        return 0

    lax.fori_loop(0, quads, step, 0)


def unpack_kernel(x_ref, o_ref):
    quads = x_ref.shape[1]

    def step(t, _):
        for u in range(4):
            tiles = [x_ref[4 * u + d, t].astype(jnp.float32) for d in range(4)]
            for i, tile in enumerate(swap_blocks(tiles)):
                o_ref[4 * t + i, :, u * LANES : (u + 1) * LANES] = tile.astype(jnp.bfloat16)
        return 0

    lax.fori_loop(0, quads, step, 0)


def observe_kernel(cells_ref, left_ref, mid_ref, right_ref, o_ref, ext):
    obs = mid_ref.shape[1]
    ext[:, :HW] = left_ref[...]
    ext[:, HW : HW + obs] = mid_ref[...]
    ext[:, HW + obs : 2 * HW + obs] = right_ref[...]
    ext[:, 2 * HW + obs :] = jnp.zeros_like(ext[:, 2 * HW + obs :])
    width = o_ref.shape[3]
    for m in range(o_ref.shape[0]):
        for g in range(o_ref.shape[1]):
            first = pl.multiple_of(cells_ref[m, g] * LANES, LANES)
            o_ref[m, g] = ext[:, pl.ds(first, width)]


def halves(a):
    hi = a.astype(jnp.bfloat16)
    return hi, (a - hi.astype(jnp.float32)).astype(jnp.bfloat16)


def product(a, b):
    (ah, al), (bh, bl) = a, b
    dot = functools.partial(jnp.dot, preferred_element_type=jnp.float32)
    return dot(ah, bh) + (dot(ah, bl) + dot(al, bh))


def across(a, b):
    return lax.dot_general(a, b, (((1,), (1,)), ((), ())), preferred_element_type=jnp.float32)


def transform_kernel(
    cells_ref, tally_ref, ens_ref, ptr_ref, val_ref, inv_ref, o_ref, yh, yl, zh, zl, norm, push
):
    sources, groups, rows, width = ens_ref.shape
    members = sources * rows
    listed = ptr_ref.shape[0]
    r_i = lax.broadcasted_iota(jnp.int32, (members, members), 0)
    c_i = lax.broadcasted_iota(jnp.int32, (members, members), 1)
    eye = (r_i == c_i).astype(jnp.float32)
    place = lax.broadcasted_iota(jnp.int32, (listed, 1), 0)
    for g in range(groups):
        first = pl.multiple_of(cells_ref[g] * LANES, LANES)
        here = ptr_ref[:, g : g + 1] - first
        here = jnp.where(place < tally_ref[g], here, -1)
        spot = lax.broadcasted_iota(jnp.int32, (listed, width), 1)
        used = jnp.sum((spot == here).astype(jnp.float32), axis=0, keepdims=True)
        weight = inv_ref[:, pl.ds(first, width)] * used
        ens = ens_ref[:, g].reshape(members, width).astype(jnp.float32)
        ens_mean = jnp.sum(ens, axis=0, keepdims=True) * (1.0 / members)
        anomaly = (ens - ens_mean).astype(jnp.bfloat16)
        scaled = halves(anomaly.astype(jnp.float32) * weight)
        gram = across(anomaly, scaled[0]) + across(anomaly, scaled[1])
        gram = gram + (members - 1) / INFLATION * eye
        pull = jnp.broadcast_to(weight * (val_ref[:, pl.ds(first, width)] - ens_mean), (8, width))
        pulled = halves(pull)
        push[g] = across(pulled[0], anomaly) + across(pulled[1], anomaly)
        frobenius = jnp.sqrt(jnp.sum(gram * gram, keepdims=True))
        norm[g] = jnp.broadcast_to(1.0 / jnp.sqrt(frobenius), norm.shape[1:])
        y = gram / frobenius
        factor = 1.5 * eye - 0.5 * y
        f = halves(factor)
        zh[g], zl[g] = f
        yh[g], yl[g] = halves(product(halves(y), f))

    def step(k, _):
        for g in range(groups):
            y, z = (yh[g], yl[g]), (zh[g], zl[g])
            f = halves(1.5 * eye - 0.5 * product(z, y))
            yh[g], yl[g] = halves(product(y, f))
            zh[g], zl[g] = halves(product(f, z))
        return 0

    lax.fori_loop(1, NS_ITERS, step, 0)
    for g in range(groups):
        scale = norm[g][:1, :1]
        root = (zh[g].astype(jnp.float32) + zl[g].astype(jnp.float32)) * scale
        r = halves(root)
        moved = product(halves(product(halves(push[g]), r)), r)
        o_ref[:, g * members : (g + 1) * members] = (
            math.sqrt(members - 1) * root + moved[:1]
        ).astype(jnp.bfloat16)


def apply_kernel(t_ref, x_ref, o_ref):
    sources, quads, rows, _ = x_ref.shape
    members = sources * rows
    lane = lax.broadcasted_iota(jnp.int32, (members, LANES), 1)
    group = (lane >> 3) & 3

    def step(t, _):
        x = x_ref[:, t].reshape(members, LANES).astype(jnp.float32)
        center = jnp.sum(x, axis=0, keepdims=True) * (1.0 / members)
        pert = x - center
        stack = jnp.concatenate(
            [jnp.where(group == g, pert, 0.0).astype(jnp.bfloat16) for g in range(4)], axis=0
        )
        moved = jnp.dot(t_ref[...], stack, preferred_element_type=jnp.float32)
        o_ref[:, t] = (center + moved).astype(jnp.bfloat16).reshape(sources, rows, LANES)
        return 0

    lax.fori_loop(0, quads, step, 0)


VM = pl.BlockSpec(memory_space=pltpu.VMEM)
SM = pl.BlockSpec(memory_space=pltpu.SMEM)


def call(kernel, out_shape, in_specs, scratch=(), flops=0, size=0):
    return pl.pallas_call(
        kernel,
        out_shape=out_shape,
        in_specs=in_specs,
        out_specs=VM,
        scratch_shapes=list(scratch),
        cost_estimate=pl.CostEstimate(flops=flops, bytes_accessed=size, transcendentals=0),
        compiler_params=pltpu.CompilerParams(vmem_limit_bytes=40 << 20),
    )


def ring(count, by):
    return [(i, (i + by) % count) for i in range(count)]


def swap(a):
    return lax.all_to_all(a, "mem", split_axis=0, concat_axis=0, tiled=True)


def per_device(prior, sensor, readings, precision, pointers, tally):
    rows, fields, columns = prior.shape
    blocks = lax.axis_size("mem")
    regions = lax.axis_size("reg")
    groups = tally.shape[2]
    members = rows * blocks
    listed = pointers.shape[3]
    width = listed + LANES
    bf16, f32 = jnp.bfloat16, jnp.float32
    quads = -(-fields // 4)
    per = quads // CHUNKS

    lists = pointers[0, 0]
    cells = jnp.min(lists, axis=1) // LANES
    all_cells = swap(jnp.broadcast_to(cells[None], (blocks, groups)))

    runs = sensor[:, 0]
    obs = runs.shape[1]
    left = lax.ppermute(runs[:, obs - HW :], "reg", ring(regions, 1))
    right = lax.ppermute(runs[:, :HW], "reg", ring(regions, -1))
    stats = jnp.concatenate([readings, precision], axis=0)
    s_left = lax.ppermute(stats[:, obs - HW :], "reg", ring(regions, 1))
    s_right = lax.ppermute(stats[:, :HW], "reg", ring(regions, -1))
    stats = jnp.concatenate([s_left, stats, s_right, jnp.zeros((2, LANES), f32)], axis=1)

    by_field = jnp.transpose(prior, (1, 0, 2))
    packed = pl.pallas_call(
        pack_kernel,
        grid=(CHUNKS,),
        out_shape=jax.ShapeDtypeStruct((blocks, quads, rows, LANES), bf16),
        in_specs=[pl.BlockSpec((4 * per, rows, columns), lambda i: (i, 0, 0))],
        out_specs=pl.BlockSpec((blocks, per, rows, LANES), lambda i: (0, i, 0, 0)),
        cost_estimate=pl.CostEstimate(flops=0, bytes_accessed=2 * 2 * prior.size, transcendentals=0),
    )(by_field)

    windows = call(
        observe_kernel,
        jax.ShapeDtypeStruct((blocks, groups, rows, width), bf16),
        [SM, VM, VM, VM],
        [pltpu.VMEM((rows, obs + 2 * HW + LANES), bf16)],
        size=4 << 20,
    )(all_cells, left, runs, right)
    windows = swap(windows)
    moved = swap(packed)

    square = (groups, members, members)
    transform = call(
        transform_kernel,
        jax.ShapeDtypeStruct((members, groups * members), bf16),
        [SM, SM, VM, VM, VM, VM],
        [pltpu.VMEM(square, bf16)] * 4
        + [pltpu.VMEM((groups, 8, LANES), f32), pltpu.VMEM((groups, 8, members), f32)],
        flops=6 << 30,
        size=4 << 20,
    )(cells, tally[0, 0], windows, lists.T, stats[:1], stats[1:])

    tile = pl.BlockSpec((blocks, per, rows, LANES), lambda i: (0, i, 0, 0))
    analysed = pl.pallas_call(
        apply_kernel,
        grid=(CHUNKS,),
        out_shape=jax.ShapeDtypeStruct((blocks, quads, rows, LANES), bf16),
        in_specs=[pl.BlockSpec((members, groups * members), lambda i: (0, 0)), tile],
        out_specs=tile,
    )(transform, moved)
    back = swap(analysed)
    out = pl.pallas_call(
        unpack_kernel,
        grid=(CHUNKS,),
        out_shape=jax.ShapeDtypeStruct((fields, rows, columns), bf16),
        in_specs=[tile],
        out_specs=pl.BlockSpec((4 * per, rows, columns), lambda i: (i, 0, 0)),
    )(back)
    return jnp.transpose(out, (1, 0, 2))


def solution(mesh):
    placed = (
        P("mem", None, "reg"),
        P("mem", "reg", None),
        P("reg", None),
        P("reg", None),
        P("reg", "mem", None, None),
        P("reg", "mem", None),
    )
    return jax.shard_map(
        per_device, mesh=mesh, in_specs=placed, out_specs=P("mem", None, "reg"), check_vma=False
    )
```

time: 245 us -> 193 us (0.79)
  Pallas kernels: 0 us -> 62.5 us
  local copies, waits for them, and re-layouts: 58.5 us -> 2.72 us
  matrix products: 29.2 us -> 0 us
  other arithmetic: 17.1 us -> 0.92 us
  between operations: 13.8 us -> 0.13 us
  waiting for transfers between devices: 61.4 us -> 50.9 us
  blocking collectives: 55.4 us -> 64.6 us
    pallas_call x0 -> x5, Pallas kernels: none -> 62.5 us  [the longest x1 21.3 us: per_device(): pl.pallas_call(apply_kernel, grid=(CHUNKS,), out_shape=jax.ShapeDtypeStru...]
    dot_general x22 -> x0, matrix products: 29.2 us -> none  [the longest x6 7.02 us: nearby_correction(): jnp.dot(inverse_root, iterate, precision=highest)]
    gather x4 -> x0, local copies, waits for them, and re-layouts: 18.3 us -> none  [the longest x2 10.2 us: per_device(): sensor_space_lines = jnp.take(gathered[:, 0], own_lists.reshape(-1), axis=1)]
    convert_element_type x4 -> x0, other arithmetic: 10.7 us -> none  [the longest x1 6.74 us: nearby_correction(): (prior_states_narrow - middle_pillar[None]).astype(jnp.bfloat16)]
    all_to_all x2 -> x0, local copies, waits for them, and re-layouts: 9.72 us -> none  [per_device(): lax.all_to_all(analysed, 'mem', split_axis=0, concat_axis=2, tiled=True)]
    all_to_all x1 -> x2, blocking collectives: 55.4 us -> 64.6 us  [swap(): return lax.all_to_all(a, 'mem', split_axis=0, concat_axis=0, tiled=True)]
    reshape x1 -> x0, local copies, waits for them, and re-layouts: 7.84 us -> none  [per_device(): analysed = analysed.reshape(runs_sequence, fields_sequence, columns_here)]
    all_gather x1 -> x0, local copies, waits for them, and re-layouts: 6.61 us -> none  [per_device(): gathered = lax.all_gather(extended, 'mem', axis=0, tiled=True)]
  transfers between devices with their start and end apart: 6 -> 6, of which waited for: 5 -> 2; matrix products, arithmetic and copies ran while one was open for 15% -> 1% of each run, Pallas kernels for 0% -> 14%
where the time goes in v1:
time: 193 us; the launch traced here: 192 us
  blocking collectives  64.6 us (33%)
  Pallas kernels  62.5 us (32%)
  waiting for transfers between devices  50.9 us (26%)
  starting transfers between devices  10.5 us (5%)
  local copies, waits for them, and re-layouts  2.72 us (1%)
    all_to_all x2, blocking collectives, swap(): return lax.all_to_all(a, 'mem', split_axis=0, concat_axis=0, tiled=True)  64.6 us
    all_to_all x2, waiting for transfers between devices, swap(): return lax.all_to_all(a, 'mem', split_axis=0, concat_axis=0, tiled=True)  50.9 us
    pallas_call x1, Pallas kernels, per_device(): pl.pallas_call(apply_kernel, grid=(CHUNKS,), out_shape=jax.ShapeDtypeStru...  21.3 us
    pallas_call x1, Pallas kernels, per_device(): call(transform_kernel, jax.ShapeDtypeStruct((members, groups * members),...  16.3 us
    pallas_call x1, Pallas kernels, per_device(): pl.pallas_call(pack_kernel, grid=(CHUNKS,), out_shape=jax.ShapeDtypeStruc...  11.6 us
    pallas_call x1, Pallas kernels, per_device(): pl.pallas_call(unpack_kernel, grid=(CHUNKS,), out_shape=jax.ShapeDtypeStr...  11.5 us
    all_to_all x2, starting transfers between devices, swap(): return lax.all_to_all(a, 'mem', split_axis=0, concat_axis=0, tiled=True)  8.21 us
  transfers between devices with their start and end apart: 6, of which 2 were waited for; matrix products, arithmetic and copies ran while one was open for 1% of the time, Pallas kernels for 14%

profile of v1, /device:TPU:96, one launch (start us, length us, event | category | flops | bytes accessed | tf_op | source)
XLA Modules:
  0.0 192.3 jit_solution(1631500007534229214)
XLA Ops:
  0.0 0.0 copy-start.5
  0.0 0.0 copy-start.3
  0.0 0.0 copy-start.4
  0.0 0.7 fusion
  0.8 0.0 collective-permute-start.1
  0.8 0.5 collective-permute-start
  1.3 0.8 reduce_min.9
  2.1 14.4 %all_to_all.23 = s32[16,1,4]{2,1,0:T(1,128)S(1)} all-to-all(s32[16,1,4]{2,1,0:T(1,128)S(1)} %broadcast_in_dim.4), channel_id=1, replica_groups=mesh['mem'=16,'reg'=16] {'mem'}, dimensions={0} | all-to-all | bytes 512 | tf_op jit(solution)/shard_map/all_to_all | solution.py:187
  16.5 0.0 collective-permute-done.1.right_ref
  16.5 0.0 collective-permute-done.left_ref
  16.5 0.0 copy-start.1
  16.5 0.9 copy-done.1
  17.5 1.9 shard_map.64
  19.4 3.7 %all-to-all-start.1 = ((bf16[16,4,16,640]{3,2,1,0:T(8,128)(2,1)}), bf16[16,4,16,640]{3,2,1,0:T(8,128)(2,1)S(1)}, u32[]{:S(2)}, u32[]{:S(2)}) async-start(bf16[16,4,16,640]{3,2,1,0:T(8,128)(2,1)} %shard_map.64), calls=%async_computation.1 | async-start | bytes 2621440 | tf_op jit(solution)/shard_map/all_to_all | solution.py:187
  23.1 0.0 copy-done.3
  23.1 0.0 copy-done.4
  23.1 1.3 collective-permute-start.2
  24.4 0.4 collective-permute-start.3
  24.9 0.0 copy-done.5
  24.9 0.1 copy.11
  25.0 11.6 %shard_map.66 = bf16[16,57,16,128]{3,2,1,0:T(8,128)(2,1)} custom-call(bf16[227,16,512]{2,1,0:T(8,128)(2,1)} %bitcast.13), custom_call_target="tpu_custom_call" | custom-call | bytes 7438336 | tf_op jit(solution)/shard_map/pallas_call | solution.py:216
  36.6 0.0 copy-start.2
  36.6 10.6 %all-to-all-done.1.ens_ref = bf16[16,4,16,640]{3,2,1,0:T(8,128)(2,1)S(1)} async-done(((bf16[16,4,16,640]{3,2,1,0:T(8,128)(2,1)}), bf16[16,4,16,640]{3,2,1,0:T(8,128)(2,1)S(1)}, u32[]{:S(2)}, u32[]{:S(2)}) %all-to-all-start.1) | async-done | bytes 1310752 | tf_op jit(solution)/shard_map/all_to_all | solution.py:187
  47.2 4.5 %all-to-all-start.2 = ((bf16[16,57,16,128]{3,2,1,0:T(8,128)(2,1)}), bf16[16,57,16,128]{3,2,1,0:T(8,128)(2,1)}, u32[]{:S(2)}, u32[]{:S(2)}) async-start(bf16[16,57,16,128]{3,2,1,0:T(8,128)(2,1)} %shard_map.66), calls=%async_computation.2 | async-start | bytes 7471104 | tf_op jit(solution)/shard_map/all_to_all | solution.py:187
  51.7 0.0 collective-permute-done.2
  51.7 0.0 collective-permute-done.3
  51.7 0.1 maximum_maximum_fusion
  51.8 0.1 fusion.1
  51.9 0.0 copy-done.2
  51.9 16.3 %shard_map.65.t_ref = bf16[256,1024]{1,0:T(8,128)(2,1)S(1)} custom-call(s32[4]{0:T(128)S(1)} %and_select_fusion.cells_ref, s32[4]{0:T(128)S(1)} %bitcast.12, bf16[16,4,16,640]{3,2,1,0:T(8,128)(2,1)S(1)} %all-to-all-done.1.ens_ref, s32[512,4]{1,0:T(8,128)S(1)} %bitcast.10, f32[1,8832]{1,0:T(1,128)S(1)} %get-tuple-element.8.val_ref, ...), custom_call_target="tpu_custom_call" | custom-call | flops 6442450944 | bytes 4194304 | tf_op jit(solution)/shard_map/pallas_call | solution.py:236
  68.2 0.0 copy-start
  68.2 0.8 copy-done
  69.0 40.3 %all-to-all-done.2.x_ref = bf16[16,57,16,128]{3,2,1,0:T(8,128)(2,1)} async-done(((bf16[16,57,16,128]{3,2,1,0:T(8,128)(2,1)}), bf16[16,57,16,128]{3,2,1,0:T(8,128)(2,1)}, u32[]{:S(2)}, u32[]{:S(2)}) %all-to-all-start.2) | async-done | bytes 3735584 | tf_op jit(solution)/shard_map/all_to_all | solution.py:187
  109.3 21.3 %shard_map.67 = bf16[16,57,16,128]{3,2,1,0:T(8,128)(2,1)} custom-call(bf16[256,1024]{1,0:T(8,128)(2,1)} %copy-done, bf16[16,57,16,128]{3,2,1,0:T(8,128)(2,1)} %all-to-all-done.2.x_ref), custom_call_target="tpu_custom_call" | custom-call | tf_op jit(solution)/shard_map/pallas_call | solution.py:247
  130.5 50.2 %all_to_all.24.x_ref = bf16[16,57,16,128]{3,2,1,0:T(8,128)(2,1)} all-to-all(bf16[16,57,16,128]{3,2,1,0:T(8,128)(2,1)} %shard_map.67), channel_id=1, replica_groups=mesh['mem'=16,'reg'=16] {'mem'}, dimensions={0} | all-to-all | bytes 7471104 | tf_op jit(solution)/shard_map/all_to_all | solution.py:187
  180.7 11.5 %shard_map.68 = bf16[227,16,512]{2,1,0:T(8,128)(2,1)} custom-call(bf16[16,57,16,128]{3,2,1,0:T(8,128)(2,1)} %all_to_all.24.x_ref), custom_call_target="tpu_custom_call" | custom-call | tf_op jit(solution)/shard_map/pallas_call | solution.py:255
  (5 shorter events, 0.0 us)
Async XLA Ops:
  0.0 24.9 %copy-start.5 = (s32[1,1,4,512]{3,2,1,0:T(4,128)S(1)}, s32[1,1,4,512]{3,2,1,0:T(4,128)}, u32[]{:S(2)}) copy-start(s32[1,1,4,512]{3,2,1,0:T(4,128)} %param.10) | copy-start | bytes 24580
  0.0 23.1 %copy-start.3 = (f32[1,8192]{1,0:T(1,128)S(1)}, f32[1,8192]{1,0:T(1,128)}, u32[]{:S(2)}) copy-start(f32[1,8192]{1,0:T(1,128)} %param.9) | copy-start | bytes 98308
  0.0 23.1 %copy-start.4 = (f32[1,8192]{1,0:T(1,128)S(1)}, f32[1,8192]{1,0:T(1,128)}, u32[]{:S(2)}) copy-start(f32[1,8192]{1,0:T(1,128)} %param.8) | copy-start | bytes 98308
  0.8 15.8 %collective-permute-start.1 = (bf16[16,256]{1,0:T(8,128)(2,1)S(1)}, bf16[16,256]{1,0:T(8,128)(2,1)S(1)}, u32[]{:S(2)}, u32[]{:S(2)}) collective-permute-start(bf16[16,256]{1,0:T(8,128)(2,1)S(1)} %get-tuple-element.5), channel_id=1, source_target_pairs={{0,15},{1,0},{2,1},{3,2},{4,3},{5,4},{6,5},{7,6},{8,7},{9,8},{10,9... | collective-permute-start | bytes 24584 | tf_op jit(solution)/shard_map/ppermute | solution.py:209
  0.8 15.8 %collective-permute-start = (bf16[16,256]{1,0:T(8,128)(2,1)S(1)}, bf16[16,256]{1,0:T(8,128)(2,1)S(1)}, u32[]{:S(2)}, u32[]{:S(2)}) collective-permute-start(bf16[16,256]{1,0:T(8,128)(2,1)S(1)} %get-tuple-element.6), channel_id=1, source_target_pairs={{0,1},{1,2},{2,3},{3,4},{4,5},{5,6},{6,7},{7,8},{8,9},{9,10},{10,1... | collective-permute-start | bytes 24584 | tf_op jit(solution)/shard_map/ppermute | solution.py:208
  16.5 1.0 copy-start.1
  19.4 27.8 %all-to-all-start.1 = ((bf16[16,4,16,640]{3,2,1,0:T(8,128)(2,1)}), bf16[16,4,16,640]{3,2,1,0:T(8,128)(2,1)S(1)}, u32[]{:S(2)}, u32[]{:S(2)}) async-start(bf16[16,4,16,640]{3,2,1,0:T(8,128)(2,1)} %shard_map.64), calls=%async_computation.1 | async-start | bytes 2621440 | tf_op jit(solution)/shard_map/all_to_all | solution.py:187
  23.1 28.6 %collective-permute-start.2 = (f32[2,256]{1,0:T(2,128)S(1)}, f32[2,256]{1,0:T(2,128)S(1)}, u32[]{:S(2)}, u32[]{:S(2)}) collective-permute-start(f32[2,256]{1,0:T(2,128)S(1)} %get-tuple-element.9), channel_id=1, source_target_pairs={{0,1},{1,2},{2,3},{3,4},{4,5},{5,6},{6,7},{7,8},{8,9},{9,10},{10,1... | collective-permute-start | bytes 6152 | tf_op jit(solution)/shard_map/ppermute | solution.py:211
  24.4 27.3 %collective-permute-start.3 = (f32[2,256]{1,0:T(2,128)S(1)}, f32[2,256]{1,0:T(2,128)S(1)}, u32[]{:S(2)}, u32[]{:S(2)}) collective-permute-start(f32[2,256]{1,0:T(2,128)S(1)} %get-tuple-element.10), channel_id=1, source_target_pairs={{0,15},{1,0},{2,1},{3,2},{4,3},{5,4},{6,5},{7,6},{8,7},{9,8},{10,9... | collective-permute-start | bytes 6152 | tf_op jit(solution)/shard_map/ppermute | solution.py:212
  36.6 15.3 %copy-start.2 = (s32[1,1,4]{2,1,0:T(1,128)S(1)}, s32[1,1,4]{2,1,0:T(1,128)}, u32[]{:S(2)}) copy-start(s32[1,1,4]{2,1,0:T(1,128)} %param.11) | copy-start | bytes 52
  47.2 62.1 %all-to-all-start.2 = ((bf16[16,57,16,128]{3,2,1,0:T(8,128)(2,1)}), bf16[16,57,16,128]{3,2,1,0:T(8,128)(2,1)}, u32[]{:S(2)}, u32[]{:S(2)}) async-start(bf16[16,57,16,128]{3,2,1,0:T(8,128)(2,1)} %shard_map.66), calls=%async_computation.2 | async-start | bytes 7471104 | tf_op jit(solution)/shard_map/all_to_all | solution.py:187
  68.2 0.8 copy-start

commit v2 on v1

v2 whole, which is shorter than its diff:
```python
import functools
import math

import jax
import jax.numpy as jnp
from jax import lax
from jax.experimental import pallas as pl
from jax.experimental.pallas import tpu as pltpu
from jax.sharding import PartitionSpec as P


NS_ITERS = 6
HW = 256
EARLY = 21
LANES = 128
INFLATION = 1.1
SIDE = 4


def trade_far(a, b, low):
    turned = pltpu.roll(jnp.where(low, b, a), 64, 1)
    return jnp.where(low, a, turned), jnp.where(low, turned, b)


def trade_near(a, b, even, shift):
    turned = pltpu.roll(jnp.where(even, b, a), shift, 1)
    return jnp.where(even, a, turned), jnp.where(even, turned, b)


def lane_masks(shape):
    lane = lax.broadcasted_iota(jnp.int32, shape, 1)
    return lane < 64, (lane & 32) == 0


def spread(count, width, step):
    def some(k, _):
        for i in range(width):
            step(k * width + i)
        return 0

    lax.fori_loop(0, count // width, some, 0)
    for i in range(count - count % width, count):
        step(i)


def spans(count):
    sizes = [6] + [12] * ((count - 6) // 12)
    rest = count - sum(sizes)
    sizes += [6] * (rest // 6) + [rest % 6] * (rest % 6 > 0)
    return [(sum(sizes[:k]), n) for k, n in enumerate(sizes)]


def pack_kernel(start, x_ref, _, o_ref, held, packed, sems, out_sems):
    low, even = lane_masks(packed.shape[2:])
    quads = packed.shape[1]
    fields = min(held.shape[0], x_ref.shape[0] - 4 * start)
    pieces = spans(quads)
    copies, outs = [], []
    for c, (q, n) in enumerate(pieces):
        rows = min(4 * n, fields - 4 * q)
        copies.append(
            pltpu.make_async_copy(
                x_ref.at[pl.ds(4 * (start + q), rows)], held.at[pl.ds(4 * q, rows)], sems.at[c]
            )
        )
        outs.append(
            pltpu.make_async_copy(
                packed.at[:, pl.ds(q, n)], o_ref.at[:, pl.ds(q, n)], out_sems.at[c]
            )
        )
    for copy in copies:
        copy.start()
    for v in range(fields, 4 * quads):
        held[v] = jnp.zeros(held.shape[1:], held.dtype)

    for copy, out, (q, count) in zip(copies, outs, pieces):
        copy.wait()

        def step(t, q=q):
            t = q + t
            for u in range(4):
                a = [held[4 * t + i, :, u * LANES : (u + 1) * LANES] for i in range(4)]
                a[0], a[2] = trade_far(a[0], a[2], low)
                a[1], a[3] = trade_far(a[1], a[3], low)
                a[0], a[1] = trade_near(a[0], a[1], even, 32)
                a[2], a[3] = trade_near(a[2], a[3], even, 32)
                for d in range(4):
                    packed[4 * u + d, t] = a[d]

        spread(count, 3, step)
        out.start()
    for out in outs:
        out.wait()


def unpack_kernel(x_ref, o_ref, held, sems):
    low, even = lane_masks(x_ref.shape[2:])
    fields, quads = o_ref.shape[0], x_ref.shape[1]
    copies = []
    for c, (q, n) in enumerate(spans(quads)):
        part = pl.ds(4 * q, min(4 * n, fields - 4 * q))
        copies.append(pltpu.make_async_copy(held.at[part], o_ref.at[part], sems.at[c]))
    for copy, (first, count) in zip(copies, spans(quads)):

        def step(t, first=first):
            t = first + t
            for u in range(4):
                a = [x_ref[4 * u + d, t] for d in range(4)]
                a[0], a[1] = trade_near(a[0], a[1], even, 96)
                a[2], a[3] = trade_near(a[2], a[3], even, 96)
                a[0], a[2] = trade_far(a[0], a[2], low)
                a[1], a[3] = trade_far(a[1], a[3], low)
                for i in range(4):
                    held[4 * t + i, :, u * LANES : (u + 1) * LANES] = a[i]

        spread(count, 3, step)
        copy.start()
    for copy in copies:
        copy.wait()


def extend_kernel(left_ref, right_ref, mid_ref, val_ref, inv_ref, ext, vals, invs, _, sems):
    rows, obs = mid_ref.shape
    ends = 2 * HW + obs
    inner = pl.ds(HW, obs)
    copies = [
        pltpu.make_async_copy(ref, to.at[:, inner], sems.at[k])
        for k, (ref, to) in enumerate(((mid_ref, ext), (val_ref, vals), (inv_ref, invs)))
    ]
    for copy in copies:
        copy.start()
    for to in (ext, vals, invs):
        to[:, ends:] = jnp.zeros_like(to[:, ends:])
    for ref, first in ((left_ref, 0), (right_ref, HW + obs)):
        ext[:, first : first + HW] = ref[:rows]
        side = ref[rows:].astype(jnp.float32)
        vals[:, first : first + HW] = side[0:1] + side[2:3]
        invs[:, first : first + HW] = side[1:2] + side[3:4]
    for copy in copies:
        copy.wait()


def choose_kernel(cells_ref, *refs):
    ext_refs, o_refs = refs[:SIDE], refs[SIDE:]
    groups = cells_ref.shape[1]
    tiles = o_refs[0].shape[1] // groups
    for a, o_ref in enumerate(o_refs):
        for g in range(groups):
            first = pl.multiple_of(cells_ref[a, g] * LANES, LANES)
            for b, ext in enumerate(ext_refs):
                for k in range(tiles):
                    o_ref[b, g * tiles + k] = ext[:, pl.ds(first + k * LANES, LANES)]


def halves(a):
    hi = a.astype(jnp.bfloat16)
    return hi, (a - hi.astype(jnp.float32)).astype(jnp.bfloat16)


def product(a, b):
    (ah, al), (bh, bl) = a, b
    dot = functools.partial(jnp.dot, preferred_element_type=jnp.float32)
    return dot(ah, bh) + (dot(ah, bl) + dot(al, bh))


def across(a, b):
    return lax.dot_general(a, b, (((1,), (1,)), ((), ())), preferred_element_type=jnp.float32)


def transform_kernel(me_ref, cells_ref, tally_ref, ptr_ref, val_ref, inv_ref, *refs):
    *ens_refs, o_ref, held, yh, yl, zh, zl, norm, push = refs
    sources, tiles, rows, _ = held.shape
    groups = cells_ref.shape[0]
    tiles //= groups
    members, width = sources * rows, tiles * LANES
    y, x = me_ref[0] >> 2, me_ref[0] & 3
    for a, ens_ref in enumerate(ens_refs):
        for b in range(SIDE):
            held[((y + a) & 3) * SIDE + ((x + b) & 3)] = ens_ref[b]
    listed = ptr_ref.shape[0]
    r_i = lax.broadcasted_iota(jnp.int32, (members, members), 0)
    c_i = lax.broadcasted_iota(jnp.int32, (members, members), 1)
    eye = (r_i == c_i).astype(jnp.float32)
    place = lax.broadcasted_iota(jnp.int32, (listed, 1), 0)
    for g in range(groups):
        first = pl.multiple_of(cells_ref[g] * LANES, LANES)
        here = ptr_ref[:, g : g + 1] - first
        here = jnp.where(place < tally_ref[g], here, -1)
        spot = lax.broadcasted_iota(jnp.int32, (listed, width), 1)
        used = jnp.sum((spot == here).astype(jnp.float32), axis=0, keepdims=True)
        weight = inv_ref[:, pl.ds(first, width)] * used
        ens = jnp.concatenate(
            [held[:, g * tiles + k].reshape(members, LANES) for k in range(tiles)], axis=1
        ).astype(jnp.float32)
        ens_mean = jnp.sum(ens, axis=0, keepdims=True) * (1.0 / members)
        anomaly = (ens - ens_mean).astype(jnp.bfloat16)
        scaled = halves(anomaly.astype(jnp.float32) * weight)
        gram = across(anomaly, scaled[0]) + across(anomaly, scaled[1])
        gram = gram + (members - 1) / INFLATION * eye
        pull = jnp.broadcast_to(weight * (val_ref[:, pl.ds(first, width)] - ens_mean), (8, width))
        pulled = halves(pull)
        push[g] = across(pulled[0], anomaly) + across(pulled[1], anomaly)
        frobenius = jnp.sqrt(jnp.sum(gram * gram, keepdims=True))
        norm[g] = jnp.broadcast_to(1.0 / jnp.sqrt(frobenius), norm.shape[1:])
        y = gram / frobenius
        factor = 1.5 * eye - 0.5 * y
        f = halves(factor)
        zh[g], zl[g] = f
        yh[g], yl[g] = halves(product(halves(y), f))

    def step(k, _):
        for g in range(groups):
            y, z = (yh[g], yl[g]), (zh[g], zl[g])
            f = halves(1.5 * eye - 0.5 * product(z, y))
            yh[g], yl[g] = halves(product(y, f))
            zh[g], zl[g] = halves(product(f, z))
        return 0

    lax.fori_loop(1, NS_ITERS, step, 0)
    for g in range(groups):
        scale = norm[g][:1, :1]
        root = (zh[g].astype(jnp.float32) + zl[g].astype(jnp.float32)) * scale
        r = halves(root)
        moved = product(halves(product(halves(push[g]), r)), r)
        o_ref[:, g * members : (g + 1) * members] = (
            math.sqrt(members - 1) * root + moved[:1]
        ).astype(jnp.bfloat16)


def apply_kernel(t_ref, x_ref, *refs):
    *done_refs, o_ref, held, sems = refs
    sources, quads, rows, _ = held.shape
    place = o_ref.shape[1] - quads
    members = sources * rows
    lane = lax.broadcasted_iota(jnp.int32, (members, LANES), 1)
    group = (lane >> 3) & 3

    def some(start, count):
        centers, stacks = [], []
        for i in range(count):
            x = held[:, start + i].reshape(members, LANES).astype(jnp.float32)
            center = jnp.sum(x, axis=0, keepdims=True) * (1.0 / members)
            pert = (x - center).astype(jnp.bfloat16)
            centers.append(center)
            stacks.append(
                jnp.concatenate(
                    [jnp.where(group == g, pert, jnp.zeros_like(pert)) for g in range(4)], axis=0
                )
            )
        moved = jnp.dot(
            t_ref[...], jnp.concatenate(stacks, axis=1), preferred_element_type=jnp.float32
        )
        for i in range(count):
            part = moved[:, i * LANES : (i + 1) * LANES]
            o_ref[:, place + start + i] = (
                (centers[i] + part).astype(jnp.bfloat16).reshape(sources, rows, LANES)
            )

    copies = [
        pltpu.make_async_copy(x_ref.at[:, pl.ds(q, n)], held.at[:, pl.ds(q, n)], sems.at[c])
        for c, (q, n) in enumerate(spans(quads))
    ]
    for copy in copies:
        copy.start()
    moves = [
        pltpu.make_async_copy(ref, o_ref.at[:, pl.ds(0, place)], sems.at[len(copies)])
        for ref in done_refs
    ]
    for copy in moves:
        copy.start()
    for copy, (q, count) in zip(copies, spans(quads)):
        copy.wait()

        def step(k, _, q=q):
            some(q + k * 6, 6)
            return 0

        lax.fori_loop(0, count // 6, step, 0)
        if count % 6:
            some(q + count - count % 6, count % 6)
    for copy in moves:
        copy.wait()


VM = pl.BlockSpec(memory_space=pltpu.VMEM)
SM = pl.BlockSpec(memory_space=pltpu.SMEM)
ANY = pl.BlockSpec(memory_space=pl.ANY)
HBM = pl.BlockSpec(memory_space=pltpu.HBM)


def call(
    kernel, out_shape, in_specs, scratch=(), flops=0, size=0, limit=58, out_specs=None, aliases=None
):
    return pl.pallas_call(
        kernel,
        out_shape=out_shape,
        in_specs=in_specs,
        out_specs=jax.tree.map(lambda _: VM, out_shape) if out_specs is None else out_specs,
        scratch_shapes=list(scratch),
        input_output_aliases=aliases or {},
        cost_estimate=pl.CostEstimate(flops=flops, bytes_accessed=size, transcendentals=0),
        compiler_params=pltpu.CompilerParams(vmem_limit_bytes=limit << 20),
    )


def ring(count, by):
    return [(i, (i + by) % count) for i in range(count)]


def swap(a):
    return lax.all_to_all(a, "mem", split_axis=0, concat_axis=0, tiled=True)


def offset(a, y, x):
    pairs = [
        (((r + y) % SIDE) * SIDE + (c + x) % SIDE, r * SIDE + c)
        for r in range(SIDE)
        for c in range(SIDE)
    ]
    return lax.ppermute(a, "mem", pairs)


def per_device(prior, sensor, readings, precision, pointers, tally):
    rows, fields, columns = prior.shape
    blocks = lax.axis_size("mem")
    regions = lax.axis_size("reg")
    groups = tally.shape[2]
    members = rows * blocks
    listed = pointers.shape[3]
    width = listed + LANES
    bf16, f32, i32 = jnp.bfloat16, jnp.float32, jnp.int32
    quads = -(-fields // 4)
    shape = lambda dims, kind: jax.ShapeDtypeStruct(dims, kind)

    runs = sensor[:, 0]
    obs = runs.shape[1]
    stats = jnp.concatenate([readings, precision], axis=0)
    ends = jnp.concatenate([stats[:, :HW], stats[:, obs - HW :]], axis=1)
    coarse = ends.astype(bf16)
    fine = (ends - coarse.astype(f32)).astype(bf16)
    ends = jnp.concatenate(
        [jnp.concatenate([runs[:, :HW], runs[:, obs - HW :]], axis=1), coarse, fine], axis=0
    )
    left = lax.ppermute(ends[:, HW:], "reg", ring(regions, 1))
    right = lax.ppermute(ends[:, :HW], "reg", ring(regions, -1))

    lists = pointers[0, 0]
    cells = jnp.min(lists, axis=1) // LANES
    grid = [offset(cells, y, 0) for y in range(1, SIDE)]
    grid = jnp.stack([cells] + grid)
    me = lax.axis_index("mem").astype(i32)[None]
    reach = obs + 2 * HW + LANES
    ext, vals, invs, token = call(
        extend_kernel,
        [shape((rows, reach), bf16)] + [shape((1, reach), f32)] * 2 + [shape((8, LANES), f32)],
        [VM, VM, HBM, HBM, HBM],
        [pltpu.SemaphoreType.DMA((3,))],
        size=1 << 20,
        limit=8,
    )(left, right, runs, readings, precision)
    exts = [ext] + [offset(ext, 0, x) for x in range(1, SIDE)]

    seen = groups * width // LANES
    chosen = call(
        choose_kernel,
        [shape((SIDE, seen, rows, LANES), bf16)] * SIDE,
        [SM] + [VM] * SIDE,
        size=4 << 20,
        limit=16,
    )(grid, *exts)
    windows = [chosen[0]] + [offset(chosen[-a % SIDE], a, 0) for a in range(1, SIDE)]

    by_field = jnp.transpose(prior, (1, 0, 2))

    def pack(start, count, after):
        pieces = len(spans(count))
        return call(
            functools.partial(pack_kernel, start),
            shape((blocks, count, rows, LANES), bf16),
            [HBM, ANY],
            [
                pltpu.VMEM((4 * count, rows, columns), bf16),
                pltpu.VMEM((blocks, count, rows, LANES), bf16),
                pltpu.SemaphoreType.DMA((pieces,)),
                pltpu.SemaphoreType.DMA((pieces,)),
            ],
            size=4 * prior.size * count // quads,
            out_specs=HBM,
        )(by_field, after)

    early = pack(0, EARLY, cells)
    late = pack(EARLY, quads - EARLY, token)
    early = swap(early)
    late, early = lax.optimization_barrier((late, early))
    late = swap(late)

    square = (groups, members, members)
    transform = call(
        transform_kernel,
        shape((members, groups * members), bf16),
        [SM, SM, SM] + [VM] * (3 + SIDE),
        [pltpu.VMEM((blocks, seen, rows, LANES), bf16)]
        + [pltpu.VMEM(square, bf16)] * 4
        + [pltpu.VMEM((groups, 8, LANES), f32), pltpu.VMEM((groups, 8, members), f32)],
        flops=6 << 30,
        size=4 << 20,
        limit=24,
    )(me, cells, tally[0, 0], lists.T, vals, invs, *windows)

    def apply(states, *done):
        count = states.shape[1]
        total = count + sum(d.shape[1] for d in done)
        pieces = len(spans(count))
        return call(
            apply_kernel,
            shape((blocks, total, rows, LANES), bf16),
            [VM, ANY] + [ANY] * len(done),
            [pltpu.VMEM((blocks, count, rows, LANES), bf16), pltpu.SemaphoreType.DMA((pieces + 1,))],
            flops=(4 << 30) * count // quads,
            size=4 * prior.size * count // quads,
            limit=20,
        )(transform, states, *done)

    first = apply(early)
    analysed = apply(late, first)
    back = swap(analysed)
    out = call(
        unpack_kernel,
        shape((fields, rows, columns), bf16),
        [VM],
        [
            pltpu.VMEM((4 * quads, rows, columns), bf16),
            pltpu.SemaphoreType.DMA((len(spans(quads)),)),
        ],
        size=4 * prior.size,
        out_specs=HBM,
        limit=20,
    )(back)
    return jnp.transpose(out, (1, 0, 2))


def solution(mesh):
    placed = (
        P("mem", None, "reg"),
        P("mem", "reg", None),
        P("reg", None),
        P("reg", None),
        P("reg", "mem", None, None),
        P("reg", "mem", None),
    )
    return jax.shard_map(
        per_device, mesh=mesh, in_specs=placed, out_specs=P("mem", None, "reg"), check_vma=False
    )
```

time: 193 us -> 186 us (0.964)
  starting transfers between devices: 10.5 us -> 40.6 us
  Pallas kernels: 62.5 us -> 36.5 us
  blocking collectives: 64.6 us -> 50 us
  local copies, waits for them, and re-layouts: 2.72 us -> 6.16 us
    all_to_all x2, waiting for transfers between devices: 50.9 us -> 13.9 us  [swap(): return lax.all_to_all(a, 'mem', split_axis=0, concat_axis=0, tiled=True)]
    ppermute x4 -> x11, waiting for transfers between devices: 0.01 us -> 36.8 us  [the longest x9 34.2 us: offset(): return lax.ppermute(a, 'mem', pairs)]
    ppermute x4 -> x11, starting transfers between devices: 2.27 us -> 29.7 us  [the longest x9 29.2 us: offset(): return lax.ppermute(a, 'mem', pairs)]
    pallas_call x5 -> x8, Pallas kernels: 62.5 us -> 36.5 us  [the longest x1 17 us: per_device(): call(transform_kernel, shape((members, groups * members), bf16), [SM, SM,...]
    all_to_all x2 -> x1, blocking collectives: 64.6 us -> 50 us  [swap(): return lax.all_to_all(a, 'mem', split_axis=0, concat_axis=0, tiled=True)]
    unnamed x13 -> x27, local copies, waits for them, and re-layouts: 1.9 us -> 6.15 us
    all_to_all x2, starting transfers between devices: 8.21 us -> 10.9 us  [swap(): return lax.all_to_all(a, 'mem', split_axis=0, concat_axis=0, tiled=True)]
  transfers between devices with their start and end apart: 6 -> 13, of which waited for: 2 -> 10; matrix products, arithmetic and copies ran while one was open for 1% -> 0% of each run, Pallas kernels for 14% -> 14%
where the time goes in v2:
time: 186 us
  waiting for transfers between devices  50.8 us (27%)
  blocking collectives  50 us (27%)
  starting transfers between devices  40.6 us (22%)
  Pallas kernels  36.5 us (20%)
  local copies, waits for them, and re-layouts  6.16 us (3%)
    all_to_all x1, blocking collectives, swap(): return lax.all_to_all(a, 'mem', split_axis=0, concat_axis=0, tiled=True)  50 us
    ppermute x9, waiting for transfers between devices, offset(): return lax.ppermute(a, 'mem', pairs)  34.2 us
    ppermute x9, starting transfers between devices, offset(): return lax.ppermute(a, 'mem', pairs)  29.2 us
    pallas_call x1, Pallas kernels, per_device(): call(transform_kernel, shape((members, groups * members), bf16), [SM, SM,...  17 us
    all_to_all x2, waiting for transfers between devices, swap(): return lax.all_to_all(a, 'mem', split_axis=0, concat_axis=0, tiled=True)  13.9 us
    all_to_all x2, starting transfers between devices, swap(): return lax.all_to_all(a, 'mem', split_axis=0, concat_axis=0, tiled=True)  10.9 us
    pallas_call x2, Pallas kernels, pack(): call(functools.partial(pack_kernel, start), shape((blocks, count, rows, L...  6.96 us
    pallas_call x2, Pallas kernels, apply(): call(apply_kernel, shape((blocks, total, rows, LANES), bf16), [VM, ANY] +...  6.64 us
  transfers between devices with their start and end apart: 13, of which 10 were waited for; matrix products, arithmetic and copies ran while one was open for 0% of the time, Pallas kernels for 14%

profile of v2, /device:TPU:96, one launch (start us, length us, event | category | flops | bytes accessed | tf_op | source)
XLA Modules:
  0.0 185.8 jit_solution(15531768637034870792)
XLA Ops:
  0.0 0.8 reduce_min.11
  0.8 0.6 and_select_fusion.1.cells_ref._
  1.4 3.1 %shard_map.68 = bf16[16,21,16,128]{3,2,1,0:T(8,128)(2,1)} custom-call(bf16[227,16,512]{2,1,0:T(8,128)(2,1)} %bitcast.23, s32[4]{0:T(128)} %and_select_fusion.1.cells_ref._), custom_call_target="tpu_custom_call" | custom-call | bytes 2740439 | tf_op jit(solution)/shard_map/pallas_call | solution.py:377
  4.5 0.0 copy-start.3
  4.5 0.0 copy-start.4
  4.5 0.0 copy-start.2
  4.5 7.2 %all-to-all-start = ((bf16[16,21,16,128]{3,2,1,0:T(8,128)(2,1)}), bf16[16,21,16,128]{3,2,1,0:T(8,128)(2,1)S(1)}, u32[]{:S(2)}, u32[]{:S(2)}) async-start(bf16[16,21,16,128]{3,2,1,0:T(8,128)(2,1)} %shard_map.68), calls=%async_computation | async-start | bytes 2752512 | tf_op jit(solution)/shard_map/all_to_all | solution.py:311
  11.8 0.0 collective-permute-start.1
  11.8 0.5 collective-permute-start
  12.3 0.9 collective-permute-done.1.right_ref
  13.2 1.7 collective-permute-done.left_ref
  15.0 0.1 shard_map.64
  15.1 0.6 copy-done.5
  15.7 3.9 %shard_map.67 = bf16[16,36,16,128]{3,2,1,0:T(8,128)(2,1)} custom-call(bf16[227,16,512]{2,1,0:T(8,128)(2,1)} %bitcast.24, f32[8,128]{1,0:T(8,128)} %copy-done.5), custom_call_target="tpu_custom_call" | custom-call | bytes 4697896 | tf_op jit(solution)/shard_map/pallas_call | solution.py:377
  19.6 0.0 copy-start.12
  19.6 0.0 copy-start.7
  19.6 13.9 %all-to-all-done.x_ref = bf16[16,21,16,128]{3,2,1,0:T(8,128)(2,1)S(1)} async-done(((bf16[16,21,16,128]{3,2,1,0:T(8,128)(2,1)}), bf16[16,21,16,128]{3,2,1,0:T(8,128)(2,1)S(1)}, u32[]{:S(2)}, u32[]{:S(2)}) %all-to-all-start) | async-done | bytes 1376288 | tf_op jit(solution)/shard_map/all_to_all | solution.py:311
  33.6 1.1 copy-done
  34.7 3.7 %all-to-all-start.1 = ((bf16[16,36,16,128]{3,2,1,0:T(8,128)(2,1)}), bf16[16,36,16,128]{3,2,1,0:T(8,128)(2,1)S(1)}, u32[]{:S(2)}, u32[]{:S(2)}) async-start(bf16[16,36,16,128]{3,2,1,0:T(8,128)(2,1)} %shard_map.67), calls=%async_computation.1 | async-start | bytes 4718592 | tf_op jit(solution)/shard_map/all_to_all | solution.py:311
  38.4 1.9 %collective-permute-start.4 = (s32[4]{0:T(128)S(1)}, s32[4]{0:T(128)S(1)}, u32[]{:S(2)}, u32[]{:S(2)}) collective-permute-start(s32[4]{0:T(128)S(1)} %copy-done.6), channel_id=1, source_target_pairs={{192,0},{208,16},{224,32},{240,48},{0,64},{16,80},{32,96},{48,112}... | collective-permute-start | bytes 56 | tf_op jit(solution)/shard_map/ppermute | solution.py:320
  40.3 2.7 %collective-permute-start.3 = (s32[4]{0:T(128)S(1)}, s32[4]{0:T(128)S(1)}, u32[]{:S(2)}, u32[]{:S(2)}) collective-permute-start(s32[4]{0:T(128)S(1)} %copy-done.6), channel_id=1, source_target_pairs={{128,0},{144,16},{160,32},{176,48},{192,64},{208,80},{224,96},{240... | collective-permute-start | bytes 56 | tf_op jit(solution)/shard_map/ppermute | solution.py:320
  43.0 1.5 collective-permute-start.7
  44.5 2.7 %collective-permute-start.6 = (bf16[16,8832]{1,0:T(8,128)(2,1)S(1)}, bf16[16,8832]{1,0:T(8,128)(2,1)S(1)}, u32[]{:S(2)}, u32[]{:S(2)}) collective-permute-start(bf16[16,8832]{1,0:T(8,128)(2,1)S(1)} %get-tuple-element.17.refs_0_), channel_id=1, source_target_pairs={{32,0},{48,16},{0,32},{16,48},{96,64},{112,80},{64,96},{80,112},{1... | collective-permute-start | bytes 847880 | tf_op jit(solution)/shard_map/ppermute | solution.py:320
  47.2 1.5 collective-permute-start.5
  48.7 1.4 collective-permute-done.4
  50.0 14.7 %collective-permute-start.2 = (s32[4]{0:T(128)S(1)}, s32[4]{0:T(128)S(1)}, u32[]{:S(2)}, u32[]{:S(2)}) collective-permute-start(s32[4]{0:T(128)S(1)} %copy-done.6), channel_id=1, source_target_pairs={{64,0},{80,16},{96,32},{112,48},{128,64},{144,80},{160,96},{176,11... | collective-permute-start | bytes 56 | tf_op jit(solution)/shard_map/ppermute | solution.py:320
  64.8 0.0 collective-permute-done.3
  64.8 1.3 collective-permute-done.2
  66.1 10.0 %collective-permute-done.7.refs_3_ = bf16[16,8832]{1,0:T(8,128)(2,1)S(1)} collective-permute-done((bf16[16,8832]{1,0:T(8,128)(2,1)S(1)}, bf16[16,8832]{1,0:T(8,128)(2,1)S(1)}, u32[]{:S(2)}, u32[]{:S(2)}) %collective-permute-start.7) | collective-permute-done | bytes 282656 | tf_op jit(solution)/shard_map/ppermute | solution.py:320
  76.1 7.6 %collective-permute-done.6.refs_2_ = bf16[16,8832]{1,0:T(8,128)(2,1)S(1)} collective-permute-done((bf16[16,8832]{1,0:T(8,128)(2,1)S(1)}, bf16[16,8832]{1,0:T(8,128)(2,1)S(1)}, u32[]{:S(2)}, u32[]{:S(2)}) %collective-permute-start.6) | collective-permute-done | bytes 282656 | tf_op jit(solution)/shard_map/ppermute | solution.py:320
  83.7 0.0 collective-permute-done.5.refs_1_
  83.7 1.7 shard_map.65
  85.4 1.7 collective-permute-start.8
  87.1 1.1 collective-permute-start.9
  88.2 1.4 collective-permute-start.10
  89.6 0.1 copy.7
  89.8 6.5 %collective-permute-done.8.refs_1_ = bf16[4,20,16,128]{3,2,1,0:T(8,128)(2,1)} collective-permute-done((bf16[4,20,16,128]{3,2,1,0:T(8,128)(2,1)}, bf16[4,20,16,128]{3,2,1,0:T(8,128)(2,1)}, u32[]{:S(2)}, u32[]{:S(2)}) %collective-permute-start.8) | collective-permute-done | bytes 327712 | tf_op jit(solution)/shard_map/ppermute | solution.py:320
  96.3 3.2 %collective-permute-done.9.refs_2_ = bf16[4,20,16,128]{3,2,1,0:T(8,128)(2,1)} collective-permute-done((bf16[4,20,16,128]{3,2,1,0:T(8,128)(2,1)}, bf16[4,20,16,128]{3,2,1,0:T(8,128)(2,1)}, u32[]{:S(2)}, u32[]{:S(2)}) %collective-permute-start.9) | collective-permute-done | bytes 327712 | tf_op jit(solution)/shard_map/ppermute | solution.py:320
  99.5 4.1 %collective-permute-done.10.refs_3_ = bf16[4,20,16,128]{3,2,1,0:T(8,128)(2,1)} collective-permute-done((bf16[4,20,16,128]{3,2,1,0:T(8,128)(2,1)S(1)}, bf16[4,20,16,128]{3,2,1,0:T(8,128)(2,1)}, u32[]{:S(2)}, u32[]{:S(2)}) %collective-permute-start.10) | collective-permute-done | bytes 327712 | tf_op jit(solution)/shard_map/ppermute | solution.py:320
  103.6 17.0 %shard_map.66.t_ref = bf16[256,1024]{1,0:T(8,128)(2,1)S(1)} custom-call(s32[1]{0:T(128)} %bitcast.me_ref, s32[4]{0:T(128)S(1)} %copy-done.6, s32[4]{0:T(128)S(1)} %bitcast.22, s32[512,4]{1,0:T(8,128)S(1)} %bitcast.21, f32[1,8832]{1,0:T(1,128)S(1)} %get-tuple-element.15.val_ref, f32[1,8832]{1,0:T(1,128)S(1)} %get-tuple-element.16.inv_ref, ...), custom_call_target="tpu_custom_call" | custom-call | flops 6442450944 | bytes 4194304 | tf_op jit(solution)/shard_map/pallas_call | solution.py:398
  120.6 2.5 %shard_map.69.refs_0_ = bf16[16,21,16,128]{3,2,1,0:T(8,128)(2,1)S(1)} custom-call(bf16[256,1024]{1,0:T(8,128)(2,1)S(1)} %shard_map.66.t_ref, bf16[16,21,16,128]{3,2,1,0:T(8,128)(2,1)S(1)} %copy-done.1), custom_call_target="tpu_custom_call" | custom-call | flops 1582356352 | bytes 2740439 | tf_op jit(solution)/shard_map/pallas_call | solution.py:414
  123.2 1.1 copy-done.8
  124.2 0.8 copy-done.10
  125.1 1.3 copy-done.9
  126.4 1.0 copy-done.11
  127.4 4.1 %shard_map.70 = bf16[16,57,16,128]{3,2,1,0:T(8,128)(2,1)S(1)} custom-call(bf16[256,1024]{1,0:T(8,128)(2,1)S(1)} %copy-done.11, bf16[16,36,16,128]{3,2,1,0:T(8,128)(2,1)S(1)} %all-to-all-done.1.x_ref, bf16[16,21,16,128]{3,2,1,0:T(8,128)(2,1)S(1)} %copy-done.9), custom_call_target="tpu_custom_call" | custom-call | flops 2712610816 | bytes 4697896 | tf_op jit(solution)/shard_map/pallas_call | solution.py:414
  131.6 50.0 %all_to_all.15.x_ref = bf16[16,57,16,128]{3,2,1,0:T(8,128)(2,1)S(1)} all-to-all(bf16[16,57,16,128]{3,2,1,0:T(8,128)(2,1)S(1)} %shard_map.70), channel_id=1, replica_groups=mesh['mem'=16,'reg'=16] {'mem'}, dimensions={0} | all-to-all | bytes 7471104 | tf_op jit(solution)/shard_map/all_to_all | solution.py:311
  181.6 4.1 %shard_map.71 = bf16[227,16,512]{2,1,0:T(8,128)(2,1)} custom-call(bf16[16,57,16,128]{3,2,1,0:T(8,128)(2,1)S(1)} %all_to_all.15.x_ref), custom_call_target="tpu_custom_call" | custom-call | bytes 7438336 | tf_op jit(solution)/shard_map/pallas_call | solution.py:427
  (22 shorter events, 0.1 us)
Async XLA Ops:
  4.5 7.2 %copy-start.3 = (f32[1,8192]{1,0:T(1,128)S(1)}, f32[1,8192]{1,0:T(1,128)}, u32[]{:S(2)}) copy-start(f32[1,8192]{1,0:T(1,128)} %inv_ref.1) | copy-start | bytes 98308
  4.5 7.2 %copy-start.4 = (f32[1,8192]{1,0:T(1,128)S(1)}, f32[1,8192]{1,0:T(1,128)}, u32[]{:S(2)}) copy-start(f32[1,8192]{1,0:T(1,128)} %val_ref.1) | copy-start | bytes 98308
  4.5 7.2 %copy-start.2 = (bf16[16,1,8192]{2,0,1:T(8,128)(2,1)S(1)}, bf16[16,1,8192]{2,0,1:T(8,128)(2,1)}, u32[]{:S(2)}) copy-start(bf16[16,1,8192]{2,0,1:T(8,128)(2,1)} %param.7) | copy-start | bytes 786436
  4.5 29.1 %all-to-all-start = ((bf16[16,21,16,128]{3,2,1,0:T(8,128)(2,1)}), bf16[16,21,16,128]{3,2,1,0:T(8,128)(2,1)S(1)}, u32[]{:S(2)}, u32[]{:S(2)}) async-start(bf16[16,21,16,128]{3,2,1,0:T(8,128)(2,1)} %shard_map.68), calls=%async_computation | async-start | bytes 2752512 | tf_op jit(solution)/shard_map/all_to_all | solution.py:311
  11.8 1.4 collective-permute-start.1
  11.8 3.1 %collective-permute-start = (bf16[20,256]{1,0:T(8,128)(2,1)S(1)}, bf16[20,256]{1,0:T(8,128)(2,1)S(1)}, u32[]{:S(2)}, u32[]{:S(2)}) collective-permute-start(bf16[20,256]{1,0:T(8,128)(2,1)S(1)} %get-tuple-element.30), channel_id=1, source_target_pairs={{0,1},{1,2},{2,3},{3,4},{4,5},{5,6},{6,7},{7,8},{8,9},{9,10},{10,1... | collective-permute-start | bytes 30728 | tf_op jit(solution)/shard_map/ppermute | solution.py:344
  15.1 0.6 copy-start.5
  19.6 18.8 %copy-start.6 = (s32[4]{0:T(128)S(1)}, s32[4]{0:T(128)}, u32[]{:S(2)}) copy-start(s32[4]{0:T(128)} %and_select_fusion.1.cells_ref._) | copy-start | bytes 52
  19.6 70.0 %copy-start.12 = (s32[1,1,4,512]{3,2,1,0:T(4,128)S(1)}, s32[1,1,4,512]{3,2,1,0:T(4,128)}, u32[]{:S(2)}) copy-start(s32[1,1,4,512]{3,2,1,0:T(4,128)} %param.10) | copy-start | bytes 24580
  19.6 84.0 %copy-start.7 = (s32[1,1,4]{2,1,0:T(1,128)S(1)}, s32[1,1,4]{2,1,0:T(1,128)}, u32[]{:S(2)}) copy-start(s32[1,1,4]{2,1,0:T(1,128)} %param.11) | copy-start | bytes 52
  33.6 1.1 copy-start
  34.7 90.4 %all-to-all-start.1 = ((bf16[16,36,16,128]{3,2,1,0:T(8,128)(2,1)}), bf16[16,36,16,128]{3,2,1,0:T(8,128)(2,1)S(1)}, u32[]{:S(2)}, u32[]{:S(2)}) async-start(bf16[16,36,16,128]{3,2,1,0:T(8,128)(2,1)} %shard_map.67), calls=%async_computation.1 | async-start | bytes 4718592 | tf_op jit(solution)/shard_map/all_to_all | solution.py:311
  38.4 11.6 %collective-permute-start.4 = (s32[4]{0:T(128)S(1)}, s32[4]{0:T(128)S(1)}, u32[]{:S(2)}, u32[]{:S(2)}) collective-permute-start(s32[4]{0:T(128)S(1)} %copy-done.6), channel_id=1, source_target_pairs={{192,0},{208,16},{224,32},{240,48},{0,64},{16,80},{32,96},{48,112}... | collective-permute-start | bytes 56 | tf_op jit(solution)/shard_map/ppermute | solution.py:320
  40.3 24.4 %collective-permute-start.3 = (s32[4]{0:T(128)S(1)}, s32[4]{0:T(128)S(1)}, u32[]{:S(2)}, u32[]{:S(2)}) collective-permute-start(s32[4]{0:T(128)S(1)} %copy-done.6), channel_id=1, source_target_pairs={{128,0},{144,16},{160,32},{176,48},{192,64},{208,80},{224,96},{240... | collective-permute-start | bytes 56 | tf_op jit(solution)/shard_map/ppermute | solution.py:320
  43.0 33.0 %collective-permute-start.7 = (bf16[16,8832]{1,0:T(8,128)(2,1)S(1)}, bf16[16,8832]{1,0:T(8,128)(2,1)S(1)}, u32[]{:S(2)}, u32[]{:S(2)}) collective-permute-start(bf16[16,8832]{1,0:T(8,128)(2,1)S(1)} %get-tuple-element.17.refs_0_), channel_id=1, source_target_pairs={{48,0},{0,16},{16,32},{32,48},{112,64},{64,80},{80,96},{96,112},{1... | collective-permute-start | bytes 847880 | tf_op jit(solution)/shard_map/ppermute | solution.py:320
  44.5 39.2 %collective-permute-start.6 = (bf16[16,8832]{1,0:T(8,128)(2,1)S(1)}, bf16[16,8832]{1,0:T(8,128)(2,1)S(1)}, u32[]{:S(2)}, u32[]{:S(2)}) collective-permute-start(bf16[16,8832]{1,0:T(8,128)(2,1)S(1)} %get-tuple-element.17.refs_0_), channel_id=1, source_target_pairs={{32,0},{48,16},{0,32},{16,48},{96,64},{112,80},{64,96},{80,112},{1... | collective-permute-start | bytes 847880 | tf_op jit(solution)/shard_map/ppermute | solution.py:320
  47.2 36.5 %collective-permute-start.5 = (bf16[16,8832]{1,0:T(8,128)(2,1)S(1)}, bf16[16,8832]{1,0:T(8,128)(2,1)S(1)}, u32[]{:S(2)}, u32[]{:S(2)}) collective-permute-start(bf16[16,8832]{1,0:T(8,128)(2,1)S(1)} %get-tuple-element.17.refs_0_), channel_id=1, source_target_pairs={{16,0},{32,16},{48,32},{0,48},{80,64},{96,80},{112,96},{64,112},{1... | collective-permute-start | bytes 847880 | tf_op jit(solution)/shard_map/ppermute | solution.py:320
  50.0 16.0 %collective-permute-start.2 = (s32[4]{0:T(128)S(1)}, s32[4]{0:T(128)S(1)}, u32[]{:S(2)}, u32[]{:S(2)}) collective-permute-start(s32[4]{0:T(128)S(1)} %copy-done.6), channel_id=1, source_target_pairs={{64,0},{80,16},{96,32},{112,48},{128,64},{144,80},{160,96},{176,11... | collective-permute-start | bytes 56 | tf_op jit(solution)/shard_map/ppermute | solution.py:320
  85.4 10.9 %collective-permute-start.8 = (bf16[4,20,16,128]{3,2,1,0:T(8,128)(2,1)}, bf16[4,20,16,128]{3,2,1,0:T(8,128)(2,1)}, u32[]{:S(2)}, u32[]{:S(2)}) collective-permute-start(bf16[4,20,16,128]{3,2,1,0:T(8,128)(2,1)} %get-tuple-element.19), channel_id=1, source_target_pairs={{64,0},{80,16},{96,32},{112,48},{128,64},{144,80},{160,96},{176,11... | collective-permute-start | bytes 983048 | tf_op jit(solution)/shard_map/ppermute | solution.py:320
  87.1 12.4 %collective-permute-start.9 = (bf16[4,20,16,128]{3,2,1,0:T(8,128)(2,1)}, bf16[4,20,16,128]{3,2,1,0:T(8,128)(2,1)}, u32[]{:S(2)}, u32[]{:S(2)}) collective-permute-start(bf16[4,20,16,128]{3,2,1,0:T(8,128)(2,1)} %get-tuple-element.20), channel_id=1, source_target_pairs={{128,0},{144,16},{160,32},{176,48},{192,64},{208,80},{224,96},{240... | collective-permute-start | bytes 983048 | tf_op jit(solution)/shard_map/ppermute | solution.py:320
  88.2 15.4 %collective-permute-start.10 = (bf16[4,20,16,128]{3,2,1,0:T(8,128)(2,1)S(1)}, bf16[4,20,16,128]{3,2,1,0:T(8,128)(2,1)}, u32[]{:S(2)}, u32[]{:S(2)}) collective-permute-start(bf16[4,20,16,128]{3,2,1,0:T(8,128)(2,1)S(1)} %get-tuple-element.21), channel_id=1, source_target_pairs={{192,0},{208,16},{224,32},{240,48},{0,64},{16,80},{32,96},{48,112}... | collective-permute-start | bytes 983048 | tf_op jit(solution)/shard_map/ppermute | solution.py:320
  103.6 17.0 %copy-start.1 = (bf16[16,21,16,128]{3,2,1,0:T(8,128)(2,1)S(1)}, bf16[16,21,16,128]{3,2,1,0:T(8,128)(2,1)}, u32[]{:S(2)}) copy-start(bf16[16,21,16,128]{3,2,1,0:T(8,128)(2,1)} %copy-done) | copy-start | bytes 4128772
  123.1 1.1 copy-start.8
  124.2 0.8 copy-start.10
  125.1 1.3 copy-start.9
  126.4 1.0 copy-start.11

commit v3 on v2

--- a/solution.py
+++ b/solution.py
@@ -11,7 +11,7 @@
 
 NS_ITERS = 6
 HW = 256
-EARLY = 21
+EARLY = 18
 LANES = 128
 INFLATION = 1.1
 SIDE = 4
@@ -50,7 +50,8 @@
     return [(sum(sizes[:k]), n) for k, n in enumerate(sizes)]
 
 
-def pack_kernel(start, x_ref, _, o_ref, held, packed, sems, out_sems):
+def pack_kernel(start, x_ref, *refs):
+    o_ref, held, packed, sems, out_sems = refs[-5:]
     low, even = lane_masks(packed.shape[2:])
     quads = packed.shape[1]
     fields = min(held.shape[0], x_ref.shape[0] - 4 * start)
@@ -65,7 +66,7 @@
         )
         outs.append(
             pltpu.make_async_copy(
-                packed.at[:, pl.ds(q, n)], o_ref.at[:, pl.ds(q, n)], out_sems.at[c]
+                packed.at[:, pl.ds(q, n)], o_ref.at[:, pl.ds(start + q, n)], out_sems.at[c]
             )
         )
     for copy in copies:
@@ -119,37 +120,43 @@
         copy.wait()
 
 
-def extend_kernel(left_ref, right_ref, mid_ref, val_ref, inv_ref, ext, vals, invs, _, sems):
+def choose_kernel(
+    cells_ref, left_ref, right_ref, val_ref, inv_ref, mid_ref, *refs
+):
+    runs_refs, side_refs = refs[: SIDE - 1], refs[SIDE - 1 : 2 * SIDE - 2]
+    *o_refs, vals, invs, ext, sems = refs[2 * SIDE - 2 :]
     rows, obs = mid_ref.shape
     ends = 2 * HW + obs
     inner = pl.ds(HW, obs)
     copies = [
         pltpu.make_async_copy(ref, to.at[:, inner], sems.at[k])
-        for k, (ref, to) in enumerate(((mid_ref, ext), (val_ref, vals), (inv_ref, invs)))
+        for k, (ref, to) in enumerate(((mid_ref, ext.at[0]), (val_ref, vals), (inv_ref, invs)))
     ]
     for copy in copies:
         copy.start()
-    for to in (ext, vals, invs):
+    for to in (vals, invs):
         to[:, ends:] = jnp.zeros_like(to[:, ends:])
     for ref, first in ((left_ref, 0), (right_ref, HW + obs)):
-        ext[:, first : first + HW] = ref[:rows]
+        ext[0, :, first : first + HW] = ref[:rows]
         side = ref[rows:].astype(jnp.float32)
         vals[:, first : first + HW] = side[0:1] + side[2:3]
         invs[:, first : first + HW] = side[1:2] + side[3:4]
+    for b in range(SIDE):
+        ext[b, :, ends:] = jnp.zeros_like(ext[b, :, ends:])
+    for b, (ref, sides) in enumerate(zip(runs_refs, side_refs)):
+        ext[b + 1, :, :HW] = sides[:, :HW]
+        ext[b + 1, :, HW : HW + obs] = ref[...]
+        ext[b + 1, :, HW + obs : ends] = sides[:, HW:]
     for copy in copies:
         copy.wait()
-
-
-def choose_kernel(cells_ref, *refs):
-    ext_refs, o_refs = refs[:SIDE], refs[SIDE:]
     groups = cells_ref.shape[1]
     tiles = o_refs[0].shape[1] // groups
     for a, o_ref in enumerate(o_refs):
         for g in range(groups):
             first = pl.multiple_of(cells_ref[a, g] * LANES, LANES)
-            for b, ext in enumerate(ext_refs):
+            for b in range(SIDE):
                 for k in range(tiles):
-                    o_ref[b, g * tiles + k] = ext[:, pl.ds(first + k * LANES, LANES)]
+                    o_ref[b, g * tiles + k] = ext[b, :, pl.ds(first + k * LANES, LANES)]
 
 
 def halves(a):
@@ -227,10 +234,8 @@
         ).astype(jnp.bfloat16)
 
 
-def apply_kernel(t_ref, x_ref, *refs):
-    *done_refs, o_ref, held, sems = refs
+def apply_kernel(t_ref, x_ref, o_ref, held, sems):
     sources, quads, rows, _ = held.shape
-    place = o_ref.shape[1] - quads
     members = sources * rows
     lane = lax.broadcasted_iota(jnp.int32, (members, LANES), 1)
     group = (lane >> 3) & 3
@@ -252,23 +257,18 @@
         )
         for i in range(count):
             part = moved[:, i * LANES : (i + 1) * LANES]
-            o_ref[:, place + start + i] = (
+            o_ref[:, start + i] = (
                 (centers[i] + part).astype(jnp.bfloat16).reshape(sources, rows, LANES)
             )
 
+    pieces = spans(quads)
     copies = [
         pltpu.make_async_copy(x_ref.at[:, pl.ds(q, n)], held.at[:, pl.ds(q, n)], sems.at[c])
-        for c, (q, n) in enumerate(spans(quads))
+        for c, (q, n) in enumerate(pieces)
     ]
     for copy in copies:
         copy.start()
-    moves = [
-        pltpu.make_async_copy(ref, o_ref.at[:, pl.ds(0, place)], sems.at[len(copies)])
-        for ref in done_refs
-    ]
-    for copy in moves:
-        copy.start()
-    for copy, (q, count) in zip(copies, spans(quads)):
+    for copy, (q, count) in zip(copies, pieces):
         copy.wait()
 
         def step(k, _, q=q):
@@ -278,8 +278,6 @@
         lax.fori_loop(0, count // 6, step, 0)
         if count % 6:
             some(q + count - count % 6, count % 6)
-    for copy in moves:
-        copy.wait()
 
 
 VM = pl.BlockSpec(memory_space=pltpu.VMEM)
@@ -299,7 +297,7 @@
         scratch_shapes=list(scratch),
         input_output_aliases=aliases or {},
         cost_estimate=pl.CostEstimate(flops=flops, bytes_accessed=size, transcendentals=0),
-        compiler_params=pltpu.CompilerParams(vmem_limit_bytes=limit << 20),
+        compiler_params=pltpu.CompilerParams(vmem_limit_bytes=int(limit * (1 << 20))),
     )
 
 
@@ -350,34 +348,29 @@
     grid = jnp.stack([cells] + grid)
     me = lax.axis_index("mem").astype(i32)[None]
     reach = obs + 2 * HW + LANES
-    ext, vals, invs, token = call(
-        extend_kernel,
-        [shape((rows, reach), bf16)] + [shape((1, reach), f32)] * 2 + [shape((8, LANES), f32)],
-        [VM, VM, HBM, HBM, HBM],
-        [pltpu.SemaphoreType.DMA((3,))],
-        size=1 << 20,
-        limit=8,
-    )(left, right, runs, readings, precision)
-    exts = [ext] + [offset(ext, 0, x) for x in range(1, SIDE)]
+    others = [offset(runs, 0, x) for x in range(1, SIDE)]
+    sides = jnp.concatenate([left[:rows], right[:rows]], axis=1)
+    sides = [offset(sides, 0, x) for x in range(1, SIDE)]
 
     seen = groups * width // LANES
-    chosen = call(
+    *chosen, vals, invs = call(
         choose_kernel,
-        [shape((SIDE, seen, rows, LANES), bf16)] * SIDE,
-        [SM] + [VM] * SIDE,
+        [shape((SIDE, seen, rows, LANES), bf16)] * SIDE + [shape((1, reach), f32)] * 2,
+        [SM, VM, VM, HBM, HBM, HBM] + [VM] * (2 * SIDE - 2),
+        [pltpu.VMEM((SIDE, rows, reach), bf16), pltpu.SemaphoreType.DMA((3,))],
         size=4 << 20,
         limit=16,
-    )(grid, *exts)
+    )(grid, left, right, readings, precision, runs, *others, *sides)
     windows = [chosen[0]] + [offset(chosen[-a % SIDE], a, 0) for a in range(1, SIDE)]
 
     by_field = jnp.transpose(prior, (1, 0, 2))
 
-    def pack(start, count, after):
+    def pack(start, count, *into):
         pieces = len(spans(count))
         return call(
             functools.partial(pack_kernel, start),
-            shape((blocks, count, rows, LANES), bf16),
-            [HBM, ANY],
+            shape((blocks, quads, rows, LANES), bf16),
+            [HBM] + [HBM] * len(into),
             [
                 pltpu.VMEM((4 * count, rows, columns), bf16),
                 pltpu.VMEM((blocks, count, rows, LANES), bf16),
@@ -386,13 +379,12 @@
             ],
             size=4 * prior.size * count // quads,
             out_specs=HBM,
-        )(by_field, after)
-
-    early = pack(0, EARLY, cells)
-    late = pack(EARLY, quads - EARLY, token)
-    early = swap(early)
-    late, early = lax.optimization_barrier((late, early))
-    late = swap(late)
+            aliases={1: 0} if into else None,
+        )(by_field, *into)
+
+    packed = pack(0, EARLY)
+    packed = pack(EARLY, quads - EARLY, packed)
+    moved = swap(packed)
 
     square = (groups, members, members)
     transform = call(
@@ -407,22 +399,18 @@
         limit=24,
     )(me, cells, tally[0, 0], lists.T, vals, invs, *windows)
 
-    def apply(states, *done):
-        count = states.shape[1]
-        total = count + sum(d.shape[1] for d in done)
-        pieces = len(spans(count))
-        return call(
-            apply_kernel,
-            shape((blocks, total, rows, LANES), bf16),
-            [VM, ANY] + [ANY] * len(done),
-            [pltpu.VMEM((blocks, count, rows, LANES), bf16), pltpu.SemaphoreType.DMA((pieces + 1,))],
-            flops=(4 << 30) * count // quads,
-            size=4 * prior.size * count // quads,
-            limit=20,
-        )(transform, states, *done)
-
-    first = apply(early)
-    analysed = apply(late, first)
+    analysed = call(
+        apply_kernel,
+        shape((blocks, quads, rows, LANES), bf16),
+        [VM, HBM],
+        [
+            pltpu.VMEM((blocks, quads, rows, LANES), bf16),
+            pltpu.SemaphoreType.DMA((len(spans(quads)),)),
+        ],
+        flops=4 << 30,
+        size=4 * prior.size,
+        limit=20,
+    )(transform, moved)
     back = swap(analysed)
     out = call(
         unpack_kernel,

time: 186 us -> 181 us (0.973)
  local copies, waits for them, and re-layouts: 6.16 us -> 0.19 us
  starting transfers between devices: 40.6 us -> 44.2 us
  waiting for transfers between devices: 50.8 us -> 48.7 us
    all_to_all x2 -> x1, waiting for transfers between devices: 13.9 us -> 0.01 us  [swap(): return lax.all_to_all(a, 'mem', split_axis=0, concat_axis=0, tiled=True)]
    ppermute x9 -> x12, waiting for transfers between devices: 34.2 us -> 47.7 us  [offset(): return lax.ppermute(a, 'mem', pairs)]
    ppermute x9 -> x12, starting transfers between devices: 29.2 us -> 36.5 us  [offset(): return lax.ppermute(a, 'mem', pairs)]
    unnamed x27 -> x11, local copies, waits for them, and re-layouts: 6.15 us -> 0.17 us
    all_to_all x2 -> x1, starting transfers between devices: 10.9 us -> 7.22 us  [swap(): return lax.all_to_all(a, 'mem', split_axis=0, concat_axis=0, tiled=True)]
    pallas_call x6 -> x4, Pallas kernels: 15.4 us -> 15.3 us  [the longest x1 7.31 us: per_device(): call(apply_kernel, shape((blocks, quads, rows, LANES), bf16), [VM, HBM],...]
  transfers between devices with their start and end apart: 13 -> 15, of which waited for: 10 -> 10; matrix products, arithmetic and copies ran while one was open for 0% -> 0% of each run, Pallas kernels for 14% -> 10%
where the time goes in v3:
time: 181 us; the launch traced here: 180 us
  blocking collectives  51 us (28%)
  waiting for transfers between devices  48.7 us (27%)
  starting transfers between devices  44.2 us (24%)
  Pallas kernels  35.7 us (20%)
    all_to_all x1, blocking collectives, swap(): return lax.all_to_all(a, 'mem', split_axis=0, concat_axis=0, tiled=True)  51 us
    ppermute x12, waiting for transfers between devices, offset(): return lax.ppermute(a, 'mem', pairs)  47.7 us
    ppermute x12, starting transfers between devices, offset(): return lax.ppermute(a, 'mem', pairs)  36.5 us
    pallas_call x1, Pallas kernels, per_device(): call(transform_kernel, shape((members, groups * members), bf16), [SM, SM,...  16.2 us
    pallas_call x1, Pallas kernels, per_device(): call(apply_kernel, shape((blocks, quads, rows, LANES), bf16), [VM, HBM],...  7.31 us
    all_to_all x1, starting transfers between devices, swap(): return lax.all_to_all(a, 'mem', split_axis=0, concat_axis=0, tiled=True)  7.22 us
    pallas_call x2, Pallas kernels, pack(): call(functools.partial(pack_kernel, start), shape((blocks, quads, rows, L...  7 us
    pallas_call x1, Pallas kernels, per_device(): call(unpack_kernel, shape((fields, rows, columns), bf16), [VM], [pltpu.VM...  4.11 us
  transfers between devices with their start and end apart: 15, of which 10 were waited for; matrix products, arithmetic and copies ran while one was open for 0% of the time, Pallas kernels for 10%

profile of v3, /device:TPU:96, one launch (start us, length us, event | category | flops | bytes accessed | tf_op | source)
XLA Modules:
  0.0 180.3 jit_solution(10214092972208200629)
XLA Ops:
  0.0 3.0 %shard_map.66.refs_0_ = bf16[16,57,16,128]{3,2,1,0:T(8,128)(2,1)} custom-call(bf16[227,16,512]{2,1,0:T(8,128)(2,1)} %bitcast.26), custom_call_target="tpu_custom_call" | custom-call | bytes 2348948 | tf_op jit(solution)/shard_map/pallas_call | solution.py:370
  3.0 4.0 %shard_map.67 = bf16[16,57,16,128]{3,2,1,0:T(8,128)(2,1)} custom-call(bf16[227,16,512]{2,1,0:T(8,128)(2,1)} %bitcast.27, bf16[16,57,16,128]{3,2,1,0:T(8,128)(2,1)} %shard_map.66.refs_0_), custom_call_target="tpu_custom_call", output_to_operand_aliasing={{}: (1, {})} | custom-call | bytes 5089387 | tf_op jit(solution)/shard_map/pallas_call | solution.py:370
  7.0 0.0 copy-start
  7.0 0.0 copy-start.1
  7.0 0.0 copy-start.2
  7.1 0.0 copy-start.4
  7.1 0.0 copy-start.3
  7.1 7.2 %all-to-all-start = ((bf16[16,57,16,128]{3,2,1,0:T(8,128)(2,1)}), bf16[16,57,16,128]{3,2,1,0:T(8,128)(2,1)}, u32[]{:S(2)}, u32[]{:S(2)}) async-start(bf16[16,57,16,128]{3,2,1,0:T(8,128)(2,1)} %shard_map.67), calls=%async_computation | async-start | bytes 7471104 | tf_op jit(solution)/shard_map/all_to_all | solution.py:309
  14.3 0.0 copy-done
  14.3 2.0 %collective-permute-start.7 = (bf16[16,8192]{1,0:T(8,128)(2,1)S(1)}, bf16[16,8192]{1,0:T(8,128)(2,1)S(1)}, u32[]{:S(2)}, u32[]{:S(2)}) collective-permute-start(bf16[16,8192]{1,0:T(8,128)(2,1)S(1)} %bitcast.19), channel_id=1, source_target_pairs={{48,0},{0,16},{16,32},{32,48},{112,64},{64,80},{80,96},{96,112},{1... | collective-permute-start | bytes 786440 | tf_op jit(solution)/shard_map/ppermute | solution.py:318
  16.3 2.7 %collective-permute-start.6 = (bf16[16,8192]{1,0:T(8,128)(2,1)S(1)}, bf16[16,8192]{1,0:T(8,128)(2,1)S(1)}, u32[]{:S(2)}, u32[]{:S(2)}) collective-permute-start(bf16[16,8192]{1,0:T(8,128)(2,1)S(1)} %bitcast.20), channel_id=1, source_target_pairs={{32,0},{48,16},{0,32},{16,48},{96,64},{112,80},{64,96},{80,112},{1... | collective-permute-start | bytes 786440 | tf_op jit(solution)/shard_map/ppermute | solution.py:318
  18.9 1.5 collective-permute-start.5
  20.4 0.0 copy-done.1
  20.4 0.0 copy-done.2
  20.5 0.0 collective-permute-start.4
  20.5 0.5 collective-permute-start.3
  21.0 0.1 reduce_min.11
  21.1 0.8 collective-permute-done.4.right_ref
  21.9 1.5 collective-permute-start.2
  23.4 0.3 collective-permute-done.3.left_ref
  23.6 0.6 collective-permute-start.10
  24.2 7.0 %collective-permute-done.2 = s32[4]{0:T(128)S(1)} collective-permute-done((s32[4]{0:T(128)S(1)}, s32[4]{0:T(128)S(1)}, u32[]{:S(2)}, u32[]{:S(2)}) %collective-permute-start.2) | collective-permute-done | bytes 48 | tf_op jit(solution)/shard_map/ppermute | solution.py:318
  31.2 3.2 %collective-permute-start.1 = (s32[4]{0:T(128)S(1)}, s32[4]{0:T(128)S(1)}, u32[]{:S(2)}, u32[]{:S(2)}) collective-permute-start(s32[4]{0:T(128)S(1)} %and_select_fusion.1.cells_ref), channel_id=1, source_target_pairs={{128,0},{144,16},{160,32},{176,48},{192,64},{208,80},{224,96},{240... | collective-permute-start | bytes 56 | tf_op jit(solution)/shard_map/ppermute | solution.py:318
  34.4 18.5 %collective-permute-done.1 = s32[4]{0:T(128)S(1)} collective-permute-done((s32[4]{0:T(128)S(1)}, s32[4]{0:T(128)S(1)}, u32[]{:S(2)}, u32[]{:S(2)}) %collective-permute-start.1) | collective-permute-done | bytes 48 | tf_op jit(solution)/shard_map/ppermute | solution.py:318
  52.9 6.1 %collective-permute-start = (s32[4]{0:T(128)S(1)}, s32[4]{0:T(128)S(1)}, u32[]{:S(2)}, u32[]{:S(2)}) collective-permute-start(s32[4]{0:T(128)S(1)} %and_select_fusion.1.cells_ref), channel_id=1, source_target_pairs={{64,0},{80,16},{96,32},{112,48},{128,64},{144,80},{160,96},{176,11... | collective-permute-start | bytes 56 | tf_op jit(solution)/shard_map/ppermute | solution.py:318
  59.0 1.3 collective-permute-done
  60.3 7.6 %collective-permute-start.9 = (bf16[16,512]{1,0:T(8,128)(2,1)S(1)}, bf16[16,512]{1,0:T(8,128)(2,1)S(1)}, u32[]{:S(2)}, u32[]{:S(2)}) collective-permute-start(bf16[16,512]{1,0:T(8,128)(2,1)S(1)} %pad_maximum_fusion.1), channel_id=1, source_target_pairs={{32,0},{48,16},{0,32},{16,48},{96,64},{112,80},{64,96},{80,112},{1... | collective-permute-start | bytes 49160 | tf_op jit(solution)/shard_map/ppermute | solution.py:318
  68.0 6.9 %collective-permute-done.10.refs_5_ = bf16[16,512]{1,0:T(8,128)(2,1)S(1)} collective-permute-done((bf16[16,512]{1,0:T(8,128)(2,1)S(1)}, bf16[16,512]{1,0:T(8,128)(2,1)S(1)}, u32[]{:S(2)}, u32[]{:S(2)}) %collective-permute-start.10) | collective-permute-done | bytes 16416 | tf_op jit(solution)/shard_map/ppermute | solution.py:318
  74.9 6.8 %collective-permute-start.8 = (bf16[16,512]{1,0:T(8,128)(2,1)S(1)}, bf16[16,512]{1,0:T(8,128)(2,1)S(1)}, u32[]{:S(2)}, u32[]{:S(2)}) collective-permute-start(bf16[16,512]{1,0:T(8,128)(2,1)S(1)} %pad_maximum_fusion.1), channel_id=1, source_target_pairs={{16,0},{32,16},{48,32},{0,48},{80,64},{96,80},{112,96},{64,112},{1... | collective-permute-start | bytes 49160 | tf_op jit(solution)/shard_map/ppermute | solution.py:318
  81.8 0.0 collective-permute-done.9.refs_4_
  81.8 1.4 collective-permute-done.8.refs_3_
  83.2 0.0 collective-permute-done.7.refs_2_
  83.2 0.0 collective-permute-done.6.refs_1_
  83.2 0.0 collective-permute-done.5.refs_0_
  83.2 1.0 shard_map.64
  84.2 2.0 %collective-permute-start.11 = (bf16[4,20,16,128]{3,2,1,0:T(8,128)(2,1)S(1)}, bf16[4,20,16,128]{3,2,1,0:T(8,128)(2,1)S(1)}, u32[]{:S(2)}, u32[]{:S(2)}) collective-permute-start(bf16[4,20,16,128]{3,2,1,0:T(8,128)(2,1)S(1)} %get-tuple-element.14), channel_id=1, source_target_pairs={{64,0},{80,16},{96,32},{112,48},{128,64},{144,80},{160,96},{176,11... | collective-permute-start | bytes 983048 | tf_op jit(solution)/shard_map/ppermute | solution.py:318
  86.2 1.3 collective-permute-start.12
  87.5 1.3 collective-permute-start.13
  88.8 0.1 copy.8
  89.0 8.8 %collective-permute-done.11.refs_1_ = bf16[4,20,16,128]{3,2,1,0:T(8,128)(2,1)S(1)} collective-permute-done((bf16[4,20,16,128]{3,2,1,0:T(8,128)(2,1)S(1)}, bf16[4,20,16,128]{3,2,1,0:T(8,128)(2,1)S(1)}, u32[]{:S(2)}, u32[]{:S(2)}) %collective-permute-start.11) | collective-permute-done | bytes 327712 | tf_op jit(solution)/shard_map/ppermute | solution.py:318
  97.8 0.2 collective-permute-done.12.refs_2_
  98.0 3.5 %collective-permute-done.13.refs_3_ = bf16[4,20,16,128]{3,2,1,0:T(8,128)(2,1)S(1)} collective-permute-done((bf16[4,20,16,128]{3,2,1,0:T(8,128)(2,1)S(1)}, bf16[4,20,16,128]{3,2,1,0:T(8,128)(2,1)S(1)}, u32[]{:S(2)}, u32[]{:S(2)}) %collective-permute-start.13) | collective-permute-done | bytes 327712 | tf_op jit(solution)/shard_map/ppermute | solution.py:318
  101.5 0.0 copy-done.3
  101.5 16.2 %shard_map.65.t_ref = bf16[256,1024]{1,0:T(8,128)(2,1)S(1)} custom-call(s32[1]{0:T(128)} %bitcast.me_ref, s32[4]{0:T(128)S(1)} %and_select_fusion.1.cells_ref, s32[4]{0:T(128)S(1)} %bitcast.25, s32[512,4]{1,0:T(8,128)S(1)} %bitcast.24, f32[1,8832]{1,0:T(1,128)S(1)} %get-tuple-element.11.val_ref, f32[1,8832]{1,0:T(1,128)S(1)} %get-tuple-element.12.inv_ref, ...), custom_call_target="tpu_custom_call" | custom-call | flops 6442450944 | bytes 4194304 | tf_op jit(solution)/shard_map/pallas_call | solution.py:390
  117.7 0.0 all-to-all-done.x_ref
  117.7 7.3 %shard_map.68 = bf16[16,57,16,128]{3,2,1,0:T(8,128)(2,1)S(1)} custom-call(bf16[256,1024]{1,0:T(8,128)(2,1)S(1)} %shard_map.65.t_ref, bf16[16,57,16,128]{3,2,1,0:T(8,128)(2,1)} %all-to-all-done.x_ref), custom_call_target="tpu_custom_call" | custom-call | flops 4294967296 | bytes 7438336 | tf_op jit(solution)/shard_map/pallas_call | solution.py:402
  125.0 51.0 %all_to_all.10.x_ref = bf16[16,57,16,128]{3,2,1,0:T(8,128)(2,1)S(1)} all-to-all(bf16[16,57,16,128]{3,2,1,0:T(8,128)(2,1)S(1)} %shard_map.68), channel_id=1, replica_groups=mesh['mem'=16,'reg'=16] {'mem'}, dimensions={0} | all-to-all | bytes 7471104 | tf_op jit(solution)/shard_map/all_to_all | solution.py:309
  176.0 4.1 %shard_map.69 = bf16[227,16,512]{2,1,0:T(8,128)(2,1)} custom-call(bf16[16,57,16,128]{3,2,1,0:T(8,128)(2,1)S(1)} %all_to_all.10.x_ref), custom_call_target="tpu_custom_call" | custom-call | bytes 7438336 | tf_op jit(solution)/shard_map/pallas_call | solution.py:415
  (11 shorter events, 0.1 us)
Async XLA Ops:
  7.0 7.3 %copy-start = (bf16[16,1,8192]{2,0,1:T(8,128)(2,1)S(1)}, bf16[16,1,8192]{2,0,1:T(8,128)(2,1)}, u32[]{:S(2)}) copy-start(bf16[16,1,8192]{2,0,1:T(8,128)(2,1)} %param.7) | copy-start | bytes 786436
  7.0 13.4 %copy-start.1 = (f32[1,8192]{1,0:T(1,128)S(1)}, f32[1,8192]{1,0:T(1,128)}, u32[]{:S(2)}) copy-start(f32[1,8192]{1,0:T(1,128)} %inv_ref.1) | copy-start | bytes 98308
  7.0 13.4 %copy-start.2 = (f32[1,8192]{1,0:T(1,128)S(1)}, f32[1,8192]{1,0:T(1,128)}, u32[]{:S(2)}) copy-start(f32[1,8192]{1,0:T(1,128)} %val_ref.1) | copy-start | bytes 98308
  7.1 13.9 %copy-start.4 = (s32[1,1,4,512]{3,2,1,0:T(4,128)S(1)}, s32[1,1,4,512]{3,2,1,0:T(4,128)}, u32[]{:S(2)}) copy-start(s32[1,1,4,512]{3,2,1,0:T(4,128)} %param.10) | copy-start | bytes 24580
  7.1 94.4 %copy-start.3 = (s32[1,1,4]{2,1,0:T(1,128)S(1)}, s32[1,1,4]{2,1,0:T(1,128)}, u32[]{:S(2)}) copy-start(s32[1,1,4]{2,1,0:T(1,128)} %param.11) | copy-start | bytes 52
  7.1 110.6 %all-to-all-start = ((bf16[16,57,16,128]{3,2,1,0:T(8,128)(2,1)}), bf16[16,57,16,128]{3,2,1,0:T(8,128)(2,1)}, u32[]{:S(2)}, u32[]{:S(2)}) async-start(bf16[16,57,16,128]{3,2,1,0:T(8,128)(2,1)} %shard_map.67), calls=%async_computation | async-start | bytes 7471104 | tf_op jit(solution)/shard_map/all_to_all | solution.py:309
  14.3 68.9 %collective-permute-start.7 = (bf16[16,8192]{1,0:T(8,128)(2,1)S(1)}, bf16[16,8192]{1,0:T(8,128)(2,1)S(1)}, u32[]{:S(2)}, u32[]{:S(2)}) collective-permute-start(bf16[16,8192]{1,0:T(8,128)(2,1)S(1)} %bitcast.19), channel_id=1, source_target_pairs={{48,0},{0,16},{16,32},{32,48},{112,64},{64,80},{80,96},{96,112},{1... | collective-permute-start | bytes 786440 | tf_op jit(solution)/shard_map/ppermute | solution.py:318
  16.3 66.9 %collective-permute-start.6 = (bf16[16,8192]{1,0:T(8,128)(2,1)S(1)}, bf16[16,8192]{1,0:T(8,128)(2,1)S(1)}, u32[]{:S(2)}, u32[]{:S(2)}) collective-permute-start(bf16[16,8192]{1,0:T(8,128)(2,1)S(1)} %bitcast.20), channel_id=1, source_target_pairs={{32,0},{48,16},{0,32},{16,48},{96,64},{112,80},{64,96},{80,112},{1... | collective-permute-start | bytes 786440 | tf_op jit(solution)/shard_map/ppermute | solution.py:318
  18.9 64.3 %collective-permute-start.5 = (bf16[16,8192]{1,0:T(8,128)(2,1)S(1)}, bf16[16,8192]{1,0:T(8,128)(2,1)S(1)}, u32[]{:S(2)}, u32[]{:S(2)}) collective-permute-start(bf16[16,8192]{1,0:T(8,128)(2,1)S(1)} %bitcast.21), channel_id=1, source_target_pairs={{16,0},{32,16},{48,32},{0,48},{80,64},{96,80},{112,96},{64,112},{1... | collective-permute-start | bytes 786440 | tf_op jit(solution)/shard_map/ppermute | solution.py:318
  20.5 1.4 collective-permute-start.4
  20.5 3.1 %collective-permute-start.3 = (bf16[20,256]{1,0:T(8,128)(2,1)S(1)}, bf16[20,256]{1,0:T(8,128)(2,1)S(1)}, u32[]{:S(2)}, u32[]{:S(2)}) collective-permute-start(bf16[20,256]{1,0:T(8,128)(2,1)S(1)} %get-tuple-element.22), channel_id=1, source_target_pairs={{0,1},{1,2},{2,3},{3,4},{4,5},{5,6},{6,7},{7,8},{8,9},{9,10},{10,1... | collective-permute-start | bytes 30728 | tf_op jit(solution)/shard_map/ppermute | solution.py:342
  21.9 9.3 %collective-permute-start.2 = (s32[4]{0:T(128)S(1)}, s32[4]{0:T(128)S(1)}, u32[]{:S(2)}, u32[]{:S(2)}) collective-permute-start(s32[4]{0:T(128)S(1)} %and_select_fusion.1.cells_ref), channel_id=1, source_target_pairs={{192,0},{208,16},{224,32},{240,48},{0,64},{16,80},{32,96},{48,112}... | collective-permute-start | bytes 56 | tf_op jit(solution)/shard_map/ppermute | solution.py:318
  23.6 51.3 %collective-permute-start.10 = (bf16[16,512]{1,0:T(8,128)(2,1)S(1)}, bf16[16,512]{1,0:T(8,128)(2,1)S(1)}, u32[]{:S(2)}, u32[]{:S(2)}) collective-permute-start(bf16[16,512]{1,0:T(8,128)(2,1)S(1)} %pad_maximum_fusion.1), channel_id=1, source_target_pairs={{48,0},{0,16},{16,32},{32,48},{112,64},{64,80},{80,96},{96,112},{1... | collective-permute-start | bytes 49160 | tf_op jit(solution)/shard_map/ppermute | solution.py:318
  31.2 21.8 %collective-permute-start.1 = (s32[4]{0:T(128)S(1)}, s32[4]{0:T(128)S(1)}, u32[]{:S(2)}, u32[]{:S(2)}) collective-permute-start(s32[4]{0:T(128)S(1)} %and_select_fusion.1.cells_ref), channel_id=1, source_target_pairs={{128,0},{144,16},{160,32},{176,48},{192,64},{208,80},{224,96},{240... | collective-permute-start | bytes 56 | tf_op jit(solution)/shard_map/ppermute | solution.py:318
  52.9 7.4 %collective-permute-start = (s32[4]{0:T(128)S(1)}, s32[4]{0:T(128)S(1)}, u32[]{:S(2)}, u32[]{:S(2)}) collective-permute-start(s32[4]{0:T(128)S(1)} %and_select_fusion.1.cells_ref), channel_id=1, source_target_pairs={{64,0},{80,16},{96,32},{112,48},{128,64},{144,80},{160,96},{176,11... | collective-permute-start | bytes 56 | tf_op jit(solution)/shard_map/ppermute | solution.py:318
  60.3 21.4 %collective-permute-start.9 = (bf16[16,512]{1,0:T(8,128)(2,1)S(1)}, bf16[16,512]{1,0:T(8,128)(2,1)S(1)}, u32[]{:S(2)}, u32[]{:S(2)}) collective-permute-start(bf16[16,512]{1,0:T(8,128)(2,1)S(1)} %pad_maximum_fusion.1), channel_id=1, source_target_pairs={{32,0},{48,16},{0,32},{16,48},{96,64},{112,80},{64,96},{80,112},{1... | collective-permute-start | bytes 49160 | tf_op jit(solution)/shard_map/ppermute | solution.py:318
  74.9 8.3 %collective-permute-start.8 = (bf16[16,512]{1,0:T(8,128)(2,1)S(1)}, bf16[16,512]{1,0:T(8,128)(2,1)S(1)}, u32[]{:S(2)}, u32[]{:S(2)}) collective-permute-start(bf16[16,512]{1,0:T(8,128)(2,1)S(1)} %pad_maximum_fusion.1), channel_id=1, source_target_pairs={{16,0},{32,16},{48,32},{0,48},{80,64},{96,80},{112,96},{64,112},{1... | collective-permute-start | bytes 49160 | tf_op jit(solution)/shard_map/ppermute | solution.py:318
  84.2 13.6 %collective-permute-start.11 = (bf16[4,20,16,128]{3,2,1,0:T(8,128)(2,1)S(1)}, bf16[4,20,16,128]{3,2,1,0:T(8,128)(2,1)S(1)}, u32[]{:S(2)}, u32[]{:S(2)}) collective-permute-start(bf16[4,20,16,128]{3,2,1,0:T(8,128)(2,1)S(1)} %get-tuple-element.14), channel_id=1, source_target_pairs={{64,0},{80,16},{96,32},{112,48},{128,64},{144,80},{160,96},{176,11... | collective-permute-start | bytes 983048 | tf_op jit(solution)/shard_map/ppermute | solution.py:318
  86.2 11.8 %collective-permute-start.12 = (bf16[4,20,16,128]{3,2,1,0:T(8,128)(2,1)S(1)}, bf16[4,20,16,128]{3,2,1,0:T(8,128)(2,1)S(1)}, u32[]{:S(2)}, u32[]{:S(2)}) collective-permute-start(bf16[4,20,16,128]{3,2,1,0:T(8,128)(2,1)S(1)} %get-tuple-element.15), channel_id=1, source_target_pairs={{128,0},{144,16},{160,32},{176,48},{192,64},{208,80},{224,96},{240... | collective-permute-start | bytes 983048 | tf_op jit(solution)/shard_map/ppermute | solution.py:318
  87.5 14.0 %collective-permute-start.13 = (bf16[4,20,16,128]{3,2,1,0:T(8,128)(2,1)S(1)}, bf16[4,20,16,128]{3,2,1,0:T(8,128)(2,1)S(1)}, u32[]{:S(2)}, u32[]{:S(2)}) collective-permute-start(bf16[4,20,16,128]{3,2,1,0:T(8,128)(2,1)S(1)} %get-tuple-element.16), channel_id=1, source_target_pairs={{192,0},{208,16},{224,32},{240,48},{0,64},{16,80},{32,96},{48,112}... | collective-permute-start | bytes 983048 | tf_op jit(solution)/shard_map/ppermute | solution.py:318

commit v4 on v3

--- a/solution.py
+++ b/solution.py
@@ -118,6 +118,25 @@
         copy.start()
     for copy in copies:
         copy.wait()
+
+
+def edges_kernel(runs_ref, val_ref, inv_ref, lists_ref, head_ref, tail_ref, cells_ref, ends, sems):
+    _, obs = runs_ref.shape
+    copies = [
+        pltpu.make_async_copy(runs_ref.at[:, pl.ds(first, HW)], ends.at[k], sems.at[k])
+        for k, first in enumerate((0, obs - HW))
+    ]
+    for copy in copies:
+        copy.start()
+    for g in range(lists_ref.shape[2]):
+        cells_ref[g] = jnp.min(lists_ref[0, 0, g : g + 1]) >> 7
+    for k, (ref, first) in enumerate(((head_ref, 0), (tail_ref, obs - HW))):
+        part = jnp.concatenate([val_ref[:, first : first + HW], inv_ref[:, first : first + HW]])
+        coarse = part.astype(jnp.bfloat16)
+        fine = part - coarse.astype(jnp.float32)
+        side = jnp.concatenate([coarse.astype(jnp.float32), fine], axis=0)
+        copies[k].wait()
+        ref[...] = jnp.concatenate([ends[k].astype(jnp.float32), side]).astype(jnp.bfloat16)
 
 
 def choose_kernel(
@@ -332,18 +351,19 @@
 
     runs = sensor[:, 0]
     obs = runs.shape[1]
-    stats = jnp.concatenate([readings, precision], axis=0)
-    ends = jnp.concatenate([stats[:, :HW], stats[:, obs - HW :]], axis=1)
-    coarse = ends.astype(bf16)
-    fine = (ends - coarse.astype(f32)).astype(bf16)
-    ends = jnp.concatenate(
-        [jnp.concatenate([runs[:, :HW], runs[:, obs - HW :]], axis=1), coarse, fine], axis=0
-    )
-    left = lax.ppermute(ends[:, HW:], "reg", ring(regions, 1))
-    right = lax.ppermute(ends[:, :HW], "reg", ring(regions, -1))
-
     lists = pointers[0, 0]
-    cells = jnp.min(lists, axis=1) // LANES
+    head, tail, cells = call(
+        edges_kernel,
+        [shape((rows + 4, HW), bf16)] * 2 + [shape((groups,), i32)],
+        [HBM, VM, VM, VM],
+        [pltpu.VMEM((2, rows, HW), bf16), pltpu.SemaphoreType.DMA((2,))],
+        size=1 << 16,
+        limit=63.89,
+        out_specs=[VM, VM, SM],
+    )(runs, readings, precision, pointers)
+    left = lax.ppermute(tail, "reg", ring(regions, 1))
+    right = lax.ppermute(head, "reg", ring(regions, -1))
+
     grid = [offset(cells, y, 0) for y in range(1, SIDE)]
     grid = jnp.stack([cells] + grid)
     me = lax.axis_index("mem").astype(i32)[None]

time: 181 us -> 183 us (1.011)
  Pallas kernels: 35.7 us -> 39.1 us
    ppermute x12, starting transfers between devices: 36.5 us -> 33.6 us  [offset(): return lax.ppermute(a, 'mem', pairs)]
    ppermute x12, waiting for transfers between devices: 47.7 us -> 45.4 us  [offset(): return lax.ppermute(a, 'mem', pairs)]
    pallas_call x0 -> x1, Pallas kernels: none -> 2.13 us  [per_device(): call(edges_kernel, [shape((rows + 4, HW), bf16)] * 2 + [shape((groups,),...]
  transfers between devices with their start and end apart: 15 -> 15, of which waited for: 10 -> 10; matrix products, arithmetic and copies ran while one was open for 0% -> 0% of each run, Pallas kernels for 10% -> 11%
where the time goes in v4:
time: 183 us
  blocking collectives  51 us (28%)
  waiting for transfers between devices  47.8 us (26%)
  starting transfers between devices  42.6 us (23%)
  Pallas kernels  39.1 us (21%)
    all_to_all x1, blocking collectives, swap(): return lax.all_to_all(a, 'mem', split_axis=0, concat_axis=0, tiled=True)  51 us
    ppermute x12, waiting for transfers between devices, offset(): return lax.ppermute(a, 'mem', pairs)  45.4 us
    ppermute x12, starting transfers between devices, offset(): return lax.ppermute(a, 'mem', pairs)  33.6 us
    pallas_call x1, Pallas kernels, per_device(): call(transform_kernel, shape((members, groups * members), bf16), [SM, SM,...  16.2 us
    pallas_call x1, Pallas kernels, per_device(): call(apply_kernel, shape((blocks, quads, rows, LANES), bf16), [VM, HBM],...  7.29 us
    all_to_all x1, starting transfers between devices, swap(): return lax.all_to_all(a, 'mem', split_axis=0, concat_axis=0, tiled=True)  7.22 us
    pallas_call x2, Pallas kernels, pack(): call(functools.partial(pack_kernel, start), shape((blocks, quads, rows, L...  7 us
    pallas_call x1, Pallas kernels, per_device(): call(unpack_kernel, shape((fields, rows, columns), bf16), [VM], [pltpu.VM...  4.11 us
  transfers between devices with their start and end apart: 15, of which 10 were waited for; matrix products, arithmetic and copies ran while one was open for 0% of the time, Pallas kernels for 11%

profile of v4, /device:TPU:96, one launch (start us, length us, event | category | flops | bytes accessed | tf_op | source)
XLA Modules:
  0.0 182.9 jit_solution(14861456130924651723)
XLA Ops:
  0.0 3.0 %shard_map.67.refs_0_ = bf16[16,57,16,128]{3,2,1,0:T(8,128)(2,1)} custom-call(bf16[227,16,512]{2,1,0:T(8,128)(2,1)} %bitcast.15), custom_call_target="tpu_custom_call" | custom-call | bytes 2348948 | tf_op jit(solution)/shard_map/pallas_call | solution.py:390
  3.0 4.0 %shard_map.68 = bf16[16,57,16,128]{3,2,1,0:T(8,128)(2,1)} custom-call(bf16[227,16,512]{2,1,0:T(8,128)(2,1)} %bitcast.16, bf16[16,57,16,128]{3,2,1,0:T(8,128)(2,1)} %shard_map.67.refs_0_), custom_call_target="tpu_custom_call", output_to_operand_aliasing={{}: (1, {})} | custom-call | bytes 5089387 | tf_op jit(solution)/shard_map/pallas_call | solution.py:390
  7.0 0.0 copy-start
  7.0 0.0 copy-start.4
  7.0 0.0 copy-start.3
  7.1 7.2 %all-to-all-start = ((bf16[16,57,16,128]{3,2,1,0:T(8,128)(2,1)}), bf16[16,57,16,128]{3,2,1,0:T(8,128)(2,1)}, u32[]{:S(2)}, u32[]{:S(2)}) async-start(bf16[16,57,16,128]{3,2,1,0:T(8,128)(2,1)} %shard_map.68), calls=%async_computation | async-start | bytes 7471104 | tf_op jit(solution)/shard_map/all_to_all | solution.py:328
  14.3 1.9 %collective-permute-start.7 = (bf16[16,8192]{1,0:T(8,128)(2,1)}, bf16[16,8192]{1,0:T(8,128)(2,1)}, u32[]{:S(2)}, u32[]{:S(2)}) collective-permute-start(bf16[16,8192]{1,0:T(8,128)(2,1)} %bitcast.1.runs_ref.mid_ref), channel_id=1, source_target_pairs={{48,0},{0,16},{16,32},{32,48},{112,64},{64,80},{80,96},{96,112},{1... | collective-permute-start | bytes 786440 | tf_op jit(solution)/shard_map/ppermute | solution.py:337
  16.2 2.7 %collective-permute-start.6 = (bf16[16,8192]{1,0:T(8,128)(2,1)}, bf16[16,8192]{1,0:T(8,128)(2,1)}, u32[]{:S(2)}, u32[]{:S(2)}) collective-permute-start(bf16[16,8192]{1,0:T(8,128)(2,1)} %bitcast.1.runs_ref.mid_ref), channel_id=1, source_target_pairs={{32,0},{48,16},{0,32},{16,48},{96,64},{112,80},{64,96},{80,112},{1... | collective-permute-start | bytes 786440 | tf_op jit(solution)/shard_map/ppermute | solution.py:337
  18.8 1.5 collective-permute-start.5
  20.3 2.1 %shard_map.64 = (bf16[20,256]{1,0:T(8,128)(2,1)}, bf16[20,256]{1,0:T(8,128)(2,1)}, s32[4]{0:T(128)}) custom-call(bf16[16,8192]{1,0:T(8,128)(2,1)} %bitcast.1.runs_ref.mid_ref, f32[1,8192]{1,0:T(1,128)} %val_ref.3, f32[1,8192]{1,0:T(1,128)} %inv_ref.3, s32[1,1,4,512]{3,2,1,0:T(4,128)} %lists_ref.1), custom_call_target="tpu_custom_call" | custom-call | bytes 65536 | tf_op jit(solution)/shard_map/pallas_call | solution.py:355
  22.4 0.0 collective-permute-start.3
  22.5 1.7 collective-permute-start.4
  24.2 1.6 collective-permute-done.3.left_ref
  25.8 0.8 collective-permute-done.4.right_ref
  26.6 0.6 collective-permute-start.10
  27.1 1.5 collective-permute-start.2
  28.6 17.2 %collective-permute-done.2 = s32[4]{0:T(128)S(1)} collective-permute-done((s32[4]{0:T(128)}, s32[4]{0:T(128)S(1)}, u32[]{:S(2)}, u32[]{:S(2)}) %collective-permute-start.2) | collective-permute-done | bytes 48 | tf_op jit(solution)/shard_map/ppermute | solution.py:337
  45.8 0.2 collective-permute-start.1
  46.0 6.9 %collective-permute-done.1 = s32[4]{0:T(128)S(1)} collective-permute-done((s32[4]{0:T(128)}, s32[4]{0:T(128)S(1)}, u32[]{:S(2)}, u32[]{:S(2)}) %collective-permute-start.1) | collective-permute-done | bytes 48 | tf_op jit(solution)/shard_map/ppermute | solution.py:337
  52.9 6.2 %collective-permute-start = (s32[4]{0:T(128)}, s32[4]{0:T(128)S(1)}, u32[]{:S(2)}, u32[]{:S(2)}) collective-permute-start(s32[4]{0:T(128)} %get-tuple-element.14.cells_ref), channel_id=1, source_target_pairs={{64,0},{80,16},{96,32},{112,48},{128,64},{144,80},{160,96},{176,11... | collective-permute-start | bytes 56 | tf_op jit(solution)/shard_map/ppermute | solution.py:337
  59.1 1.5 collective-permute-done
  60.6 7.8 %collective-permute-start.9 = (bf16[16,512]{1,0:T(8,128)(2,1)S(1)}, bf16[16,512]{1,0:T(8,128)(2,1)S(1)}, u32[]{:S(2)}, u32[]{:S(2)}) collective-permute-start(bf16[16,512]{1,0:T(8,128)(2,1)S(1)} %pad_maximum_fusion), channel_id=1, source_target_pairs={{32,0},{48,16},{0,32},{16,48},{96,64},{112,80},{64,96},{80,112},{1... | collective-permute-start | bytes 49160 | tf_op jit(solution)/shard_map/ppermute | solution.py:337
  68.4 6.5 %collective-permute-done.10.refs_5_ = bf16[16,512]{1,0:T(8,128)(2,1)S(1)} collective-permute-done((bf16[16,512]{1,0:T(8,128)(2,1)S(1)}, bf16[16,512]{1,0:T(8,128)(2,1)S(1)}, u32[]{:S(2)}, u32[]{:S(2)}) %collective-permute-start.10) | collective-permute-done | bytes 16416 | tf_op jit(solution)/shard_map/ppermute | solution.py:337
  74.9 6.8 %collective-permute-start.8 = (bf16[16,512]{1,0:T(8,128)(2,1)S(1)}, bf16[16,512]{1,0:T(8,128)(2,1)S(1)}, u32[]{:S(2)}, u32[]{:S(2)}) collective-permute-start(bf16[16,512]{1,0:T(8,128)(2,1)S(1)} %pad_maximum_fusion), channel_id=1, source_target_pairs={{16,0},{32,16},{48,32},{0,48},{80,64},{96,80},{112,96},{64,112},{1... | collective-permute-start | bytes 49160 | tf_op jit(solution)/shard_map/ppermute | solution.py:337
  81.7 0.6 pad_add_fusion.cells_ref
  82.4 0.0 collective-permute-done.9.refs_4_
  82.4 0.8 collective-permute-done.8.refs_3_
  83.2 0.0 collective-permute-done.7.refs_2_
  83.2 0.0 collective-permute-done.6.refs_1_
  83.2 0.0 collective-permute-done.5.refs_0_
  83.2 0.0 copy-done
  83.2 0.0 copy-start.1
  83.2 0.7 copy-done.1
  84.0 2.4 %shard_map.65 = (bf16[4,20,16,128]{3,2,1,0:T(8,128)(2,1)S(1)}, bf16[4,20,16,128]{3,2,1,0:T(8,128)(2,1)S(1)}, bf16[4,20,16,128]{3,2,1,0:T(8,128)(2,1)S(1)}, bf16[...) custom-call(s32[4,4]{1,0:T(4,128)S(1)} %pad_add_fusion.cells_ref, ...), custom_call_target="tpu_custom_call" | custom-call | bytes 4194304 | tf_op jit(solution)/shard_map/pallas_call | solution.py:376
  86.3 2.0 %collective-permute-start.11 = (bf16[4,20,16,128]{3,2,1,0:T(8,128)(2,1)S(1)}, bf16[4,20,16,128]{3,2,1,0:T(8,128)(2,1)S(1)}, u32[]{:S(2)}, u32[]{:S(2)}) collective-permute-start(bf16[4,20,16,128]{3,2,1,0:T(8,128)(2,1)S(1)} %get-tuple-element.20), channel_id=1, source_target_pairs={{64,0},{80,16},{96,32},{112,48},{128,64},{144,80},{160,96},{176,11... | collective-permute-start | bytes 983048 | tf_op jit(solution)/shard_map/ppermute | solution.py:337
  88.3 1.3 collective-permute-start.12
  89.6 1.3 collective-permute-start.13
  90.9 0.1 copy.8
  91.1 8.8 %collective-permute-done.11.refs_1_ = bf16[4,20,16,128]{3,2,1,0:T(8,128)(2,1)S(1)} collective-permute-done((bf16[4,20,16,128]{3,2,1,0:T(8,128)(2,1)S(1)}, bf16[4,20,16,128]{3,2,1,0:T(8,128)(2,1)S(1)}, u32[]{:S(2)}, u32[]{:S(2)}) %collective-permute-start.11) | collective-permute-done | bytes 327712 | tf_op jit(solution)/shard_map/ppermute | solution.py:337
  99.9 0.2 collective-permute-done.12.refs_2_
  100.1 3.5 %collective-permute-done.13.refs_3_ = bf16[4,20,16,128]{3,2,1,0:T(8,128)(2,1)S(1)} collective-permute-done((bf16[4,20,16,128]{3,2,1,0:T(8,128)(2,1)S(1)}, bf16[4,20,16,128]{3,2,1,0:T(8,128)(2,1)S(1)}, u32[]{:S(2)}, u32[]{:S(2)}) %collective-permute-start.13) | collective-permute-done | bytes 327712 | tf_op jit(solution)/shard_map/ppermute | solution.py:337
  103.6 0.0 copy-done.3
  103.6 0.6 copy-done.2
  104.2 16.2 %shard_map.66.t_ref = bf16[256,1024]{1,0:T(8,128)(2,1)S(1)} custom-call(s32[1]{0:T(128)} %bitcast.me_ref, s32[4]{0:T(128)S(1)} %copy-done.2, s32[4]{0:T(128)S(1)} %bitcast.14, s32[512,4]{1,0:T(8,128)S(1)} %bitcast.12, f32[1,8832]{1,0:T(1,128)S(1)} %get-tuple-element.17.val_ref, f32[1,8832]{1,0:T(1,128)S(1)} %get-tuple-element.18.inv_ref, ...), custom_call_target="tpu_custom_call" | custom-call | flops 6442450944 | bytes 4194304 | tf_op jit(solution)/shard_map/pallas_call | solution.py:410
  120.4 0.0 all-to-all-done.x_ref
  120.4 7.3 %shard_map.69 = bf16[16,57,16,128]{3,2,1,0:T(8,128)(2,1)S(1)} custom-call(bf16[256,1024]{1,0:T(8,128)(2,1)S(1)} %shard_map.66.t_ref, bf16[16,57,16,128]{3,2,1,0:T(8,128)(2,1)} %all-to-all-done.x_ref), custom_call_target="tpu_custom_call" | custom-call | flops 4294967296 | bytes 7438336 | tf_op jit(solution)/shard_map/pallas_call | solution.py:422
  127.7 51.0 %all_to_all.10.x_ref = bf16[16,57,16,128]{3,2,1,0:T(8,128)(2,1)S(1)} all-to-all(bf16[16,57,16,128]{3,2,1,0:T(8,128)(2,1)S(1)} %shard_map.69), channel_id=1, replica_groups=mesh['mem'=16,'reg'=16] {'mem'}, dimensions={0} | all-to-all | bytes 7471104 | tf_op jit(solution)/shard_map/all_to_all | solution.py:328
  178.7 4.1 %shard_map.70 = bf16[227,16,512]{2,1,0:T(8,128)(2,1)} custom-call(bf16[16,57,16,128]{3,2,1,0:T(8,128)(2,1)S(1)} %all_to_all.10.x_ref), custom_call_target="tpu_custom_call" | custom-call | bytes 7438336 | tf_op jit(solution)/shard_map/pallas_call | solution.py:435
  (5 shorter events, 0.0 us)
Async XLA Ops:
  7.0 76.2 %copy-start = (f32[1,8192]{1,0:T(1,128)S(1)}, f32[1,8192]{1,0:T(1,128)}, u32[]{:S(2)}) copy-start(f32[1,8192]{1,0:T(1,128)} %val_ref.3) | copy-start | bytes 98308
  7.0 83.9 %copy-start.4 = (s32[1,1,4,512]{3,2,1,0:T(4,128)S(1)}, s32[1,1,4,512]{3,2,1,0:T(4,128)}, u32[]{:S(2)}) copy-start(s32[1,1,4,512]{3,2,1,0:T(4,128)} %lists_ref.1) | copy-start | bytes 24580
  7.0 96.5 %copy-start.3 = (s32[1,1,4]{2,1,0:T(1,128)S(1)}, s32[1,1,4]{2,1,0:T(1,128)}, u32[]{:S(2)}) copy-start(s32[1,1,4]{2,1,0:T(1,128)} %param.11) | copy-start | bytes 52
  7.1 113.4 %all-to-all-start = ((bf16[16,57,16,128]{3,2,1,0:T(8,128)(2,1)}), bf16[16,57,16,128]{3,2,1,0:T(8,128)(2,1)}, u32[]{:S(2)}, u32[]{:S(2)}) async-start(bf16[16,57,16,128]{3,2,1,0:T(8,128)(2,1)} %shard_map.68), calls=%async_computation | async-start | bytes 7471104 | tf_op jit(solution)/shard_map/all_to_all | solution.py:328
  14.3 68.9 %collective-permute-start.7 = (bf16[16,8192]{1,0:T(8,128)(2,1)}, bf16[16,8192]{1,0:T(8,128)(2,1)}, u32[]{:S(2)}, u32[]{:S(2)}) collective-permute-start(bf16[16,8192]{1,0:T(8,128)(2,1)} %bitcast.1.runs_ref.mid_ref), channel_id=1, source_target_pairs={{48,0},{0,16},{16,32},{32,48},{112,64},{64,80},{80,96},{96,112},{1... | collective-permute-start | bytes 786440 | tf_op jit(solution)/shard_map/ppermute | solution.py:337
  16.2 67.0 %collective-permute-start.6 = (bf16[16,8192]{1,0:T(8,128)(2,1)}, bf16[16,8192]{1,0:T(8,128)(2,1)}, u32[]{:S(2)}, u32[]{:S(2)}) collective-permute-start(bf16[16,8192]{1,0:T(8,128)(2,1)} %bitcast.1.runs_ref.mid_ref), channel_id=1, source_target_pairs={{32,0},{48,16},{0,32},{16,48},{96,64},{112,80},{64,96},{80,112},{1... | collective-permute-start | bytes 786440 | tf_op jit(solution)/shard_map/ppermute | solution.py:337
  18.8 64.3 %collective-permute-start.5 = (bf16[16,8192]{1,0:T(8,128)(2,1)}, bf16[16,8192]{1,0:T(8,128)(2,1)}, u32[]{:S(2)}, u32[]{:S(2)}) collective-permute-start(bf16[16,8192]{1,0:T(8,128)(2,1)} %bitcast.1.runs_ref.mid_ref), channel_id=1, source_target_pairs={{16,0},{32,16},{48,32},{0,48},{80,64},{96,80},{112,96},{64,112},{1... | collective-permute-start | bytes 786440 | tf_op jit(solution)/shard_map/ppermute | solution.py:337
  22.4 3.3 %collective-permute-start.3 = (bf16[20,256]{1,0:T(8,128)(2,1)}, bf16[20,256]{1,0:T(8,128)(2,1)S(1)}, u32[]{:S(2)}, u32[]{:S(2)}) collective-permute-start(bf16[20,256]{1,0:T(8,128)(2,1)} %get-tuple-element.15), channel_id=1, source_target_pairs={{0,1},{1,2},{2,3},{3,4},{4,5},{5,6},{6,7},{7,8},{8,9},{9,10},{10,1... | collective-permute-start | bytes 30728 | tf_op jit(solution)/shard_map/ppermute | solution.py:364
  22.5 4.1 %collective-permute-start.4 = (bf16[20,256]{1,0:T(8,128)(2,1)}, bf16[20,256]{1,0:T(8,128)(2,1)S(1)}, u32[]{:S(2)}, u32[]{:S(2)}) collective-permute-start(bf16[20,256]{1,0:T(8,128)(2,1)} %get-tuple-element.16), channel_id=1, source_target_pairs={{0,15},{1,0},{2,1},{3,2},{4,3},{5,4},{6,5},{7,6},{8,7},{9,8},{10,9... | collective-permute-start | bytes 30728 | tf_op jit(solution)/shard_map/ppermute | solution.py:365
  26.6 48.3 %collective-permute-start.10 = (bf16[16,512]{1,0:T(8,128)(2,1)S(1)}, bf16[16,512]{1,0:T(8,128)(2,1)S(1)}, u32[]{:S(2)}, u32[]{:S(2)}) collective-permute-start(bf16[16,512]{1,0:T(8,128)(2,1)S(1)} %pad_maximum_fusion), channel_id=1, source_target_pairs={{48,0},{0,16},{16,32},{32,48},{112,64},{64,80},{80,96},{96,112},{1... | collective-permute-start | bytes 49160 | tf_op jit(solution)/shard_map/ppermute | solution.py:337
  27.1 18.6 %collective-permute-start.2 = (s32[4]{0:T(128)}, s32[4]{0:T(128)S(1)}, u32[]{:S(2)}, u32[]{:S(2)}) collective-permute-start(s32[4]{0:T(128)} %get-tuple-element.14.cells_ref), channel_id=1, source_target_pairs={{192,0},{208,16},{224,32},{240,48},{0,64},{16,80},{32,96},{48,112}... | collective-permute-start | bytes 56 | tf_op jit(solution)/shard_map/ppermute | solution.py:337
  45.8 7.1 %collective-permute-start.1 = (s32[4]{0:T(128)}, s32[4]{0:T(128)S(1)}, u32[]{:S(2)}, u32[]{:S(2)}) collective-permute-start(s32[4]{0:T(128)} %get-tuple-element.14.cells_ref), channel_id=1, source_target_pairs={{128,0},{144,16},{160,32},{176,48},{192,64},{208,80},{224,96},{240... | collective-permute-start | bytes 56 | tf_op jit(solution)/shard_map/ppermute | solution.py:337
  52.9 7.7 %collective-permute-start = (s32[4]{0:T(128)}, s32[4]{0:T(128)S(1)}, u32[]{:S(2)}, u32[]{:S(2)}) collective-permute-start(s32[4]{0:T(128)} %get-tuple-element.14.cells_ref), channel_id=1, source_target_pairs={{64,0},{80,16},{96,32},{112,48},{128,64},{144,80},{160,96},{176,11... | collective-permute-start | bytes 56 | tf_op jit(solution)/shard_map/ppermute | solution.py:337
  60.6 21.8 %collective-permute-start.9 = (bf16[16,512]{1,0:T(8,128)(2,1)S(1)}, bf16[16,512]{1,0:T(8,128)(2,1)S(1)}, u32[]{:S(2)}, u32[]{:S(2)}) collective-permute-start(bf16[16,512]{1,0:T(8,128)(2,1)S(1)} %pad_maximum_fusion), channel_id=1, source_target_pairs={{32,0},{48,16},{0,32},{16,48},{96,64},{112,80},{64,96},{80,112},{1... | collective-permute-start | bytes 49160 | tf_op jit(solution)/shard_map/ppermute | solution.py:337
  74.9 8.3 %collective-permute-start.8 = (bf16[16,512]{1,0:T(8,128)(2,1)S(1)}, bf16[16,512]{1,0:T(8,128)(2,1)S(1)}, u32[]{:S(2)}, u32[]{:S(2)}) collective-permute-start(bf16[16,512]{1,0:T(8,128)(2,1)S(1)} %pad_maximum_fusion), channel_id=1, source_target_pairs={{16,0},{32,16},{48,32},{0,48},{80,64},{96,80},{112,96},{64,112},{1... | collective-permute-start | bytes 49160 | tf_op jit(solution)/shard_map/ppermute | solution.py:337
  83.2 0.8 copy-start.1
  86.3 13.6 %collective-permute-start.11 = (bf16[4,20,16,128]{3,2,1,0:T(8,128)(2,1)S(1)}, bf16[4,20,16,128]{3,2,1,0:T(8,128)(2,1)S(1)}, u32[]{:S(2)}, u32[]{:S(2)}) collective-permute-start(bf16[4,20,16,128]{3,2,1,0:T(8,128)(2,1)S(1)} %get-tuple-element.20), channel_id=1, source_target_pairs={{64,0},{80,16},{96,32},{112,48},{128,64},{144,80},{160,96},{176,11... | collective-permute-start | bytes 983048 | tf_op jit(solution)/shard_map/ppermute | solution.py:337
  88.3 11.8 %collective-permute-start.12 = (bf16[4,20,16,128]{3,2,1,0:T(8,128)(2,1)S(1)}, bf16[4,20,16,128]{3,2,1,0:T(8,128)(2,1)S(1)}, u32[]{:S(2)}, u32[]{:S(2)}) collective-permute-start(bf16[4,20,16,128]{3,2,1,0:T(8,128)(2,1)S(1)} %get-tuple-element.21), channel_id=1, source_target_pairs={{128,0},{144,16},{160,32},{176,48},{192,64},{208,80},{224,96},{240... | collective-permute-start | bytes 983048 | tf_op jit(solution)/shard_map/ppermute | solution.py:337
  89.6 14.0 %collective-permute-start.13 = (bf16[4,20,16,128]{3,2,1,0:T(8,128)(2,1)S(1)}, bf16[4,20,16,128]{3,2,1,0:T(8,128)(2,1)S(1)}, u32[]{:S(2)}, u32[]{:S(2)}) collective-permute-start(bf16[4,20,16,128]{3,2,1,0:T(8,128)(2,1)S(1)} %get-tuple-element.22), channel_id=1, source_target_pairs={{192,0},{208,16},{224,32},{240,48},{0,64},{16,80},{32,96},{48,112}... | collective-permute-start | bytes 983048 | tf_op jit(solution)/shard_map/ppermute | solution.py:337
  103.6 0.6 copy-start.2
